TPU v7x, 512 devices: a whole 4x4x16 slice. The times are simulated.
512 devices in a mesh: dp: 8 (over z_lo), expert: 64 (over z_hi, y, x, core).
Axes of the slice: x: 4, y: 4, z: 16 (z_hi: 2, z_lo: 8; z = z_hi * 8 + z_lo), core: 2. Of those that a mesh axis runs over, the one named last changes fastest.
Arguments:
- route_ids: int32 [8192, 8], P(('dp', 'expert')), may hold values from 0 to 63, all different within a row; in each aligned block of 16 rows (0 to 15, 16 to 31, ...) at most 4 rows name the same one
- route_probs: float32 [8192, 8], P(('dp', 'expert')), may hold values from 0.02 to 0.25
- hidden: bfloat16 [8192, 8, 768], P(('dp', 'expert')), may hold values from -6 to 6
- upstream: bfloat16 [8192, 2048], P(('dp', 'expert')), may hold values from -6 to 6
- placement: int32 [64], replicated, may hold values from 0 to 63, each once
- swap_flags: int32 [64], replicated, may hold values from 0 to 1, as said below
- weights: bfloat16 [64, 768, 2048], P('expert', 'dp'), may hold values from -0.21875 to 0.21875
- moment1: float32 [64, 768, 2048], P('expert', 'dp'), may hold values from -24 to 24
- moment2: float32 [64, 768, 2048], P('expert', 'dp'), may hold values from 4 to 100
Outputs:
- layer_out: bfloat16 [8192, 2048], P(('dp', 'expert'))
- hidden_grads: bfloat16 [8192, 8, 768], P(('dp', 'expert'))
- new_weights: bfloat16 [64, 768, 2048], P('expert', 'dp')
- new_moment1: float32 [64, 768, 2048], P('expert', 'dp')
- new_moment2: float32 [64, 768, 2048], P('expert', 'dp')
Inputs may be any that keep to these rules, and one draw needn't show every extreme that they name: `route_ids`: within the rows of one device no expert is named more than 4 times, a bound that some block reaches. `placement`: A permutation of the expert-axis indices. swap_flags[i] equals swap_flags[(i + 32) mod 64], so trades are mutual between indices half the axis apart; swap_flags[0] and swap_flags[31] are 1.
All inputs are finite; a program needn't handle non-finite values.
Results may differ from a plain program's by a relative error of at most 0.006.
Values may be sent and summed in bfloat16 or wider, within the bound.
No kernel may reach another device: no remote copies, remote signals or barrier semaphores. Data moves between devices by JAX's collectives and lax.ppermute only.
A program may use at most 64 MiB of HBM per device.

v0:
```python
import jax
import jax.numpy as jnp
from jax import lax
from jax.sharding import PartitionSpec as P

decay_one = 0.9
decay_two = 0.95
learn_rate = 0.01
bias_one = 1.0 - 0.9**10
bias_two = 1.0 - 0.95**10
epsilon = 1e-08


def partner(block, axis, apart):
    count = lax.axis_size(axis)
    route = []
    for low in range(count):
        high = low | 1 << apart
        if high != low and high < count:
            route += [(low, high), (high, low)]
    return lax.ppermute(block, axis, route)


def adam_update(weight, first, second, gradient):
    new_first = decay_one * first + (1.0 - decay_one) * gradient
    new_second = decay_two * second + (1.0 - decay_two) * gradient * gradient
    step_size = learn_rate * (new_first / bias_one) / (jnp.sqrt(new_second / bias_two) + epsilon)
    return ((weight.astype(jnp.float32) - step_size).astype(jnp.bfloat16), new_first, new_second)


def table_lookup(lookup_table, positions):
    iota_slots = jnp.arange(lookup_table.shape[0], dtype=jnp.int32)
    matches = positions[..., None] == iota_slots
    return jnp.sum(jnp.where(matches, lookup_table, 0), axis=-1)


def shards(
    route_ids, route_probs, hidden, upstream, placement, swap_flags, weights, moment1, moment2
):
    group_size = lax.axis_size("expert")
    my_index = lax.axis_index("expert")
    top_bit = group_size.bit_length() - 2
    tokens_here, chosen = route_ids.shape
    width = upstream.shape[1]
    hidden_width = hidden.shape[2]
    total_rows = tokens_here * chosen
    capacity = 2 * total_rows // group_size
    flip_mine = table_lookup(swap_flags, my_index)
    weights_now, first_now, second_now = (weights, moment1, moment2)
    target = table_lookup(placement, route_ids.reshape(-1))
    slot_iota = jnp.arange(group_size, dtype=jnp.int32)
    onehot = (target[:, None] == slot_iota[None, :]).astype(jnp.int32)
    rank = jnp.sum((jnp.cumsum(onehot, axis=0) - onehot) * onehot, axis=1)
    position = target * capacity + rank
    full_weights = lax.all_gather(weights_now[0], "dp", axis=0, tiled=True)
    send_hidden = jnp.zeros((group_size * capacity, hidden_width), jnp.bfloat16)
    send_hidden = send_hidden.at[position].set(hidden.reshape(total_rows, hidden_width))
    send_hidden = send_hidden.reshape(group_size, capacity, hidden_width)
    received = lax.all_to_all(send_hidden, "expert", split_axis=0, concat_axis=0, tiled=True)
    product = jnp.einsum(
        "sch,hd->scd", received, full_weights, preferred_element_type=jnp.float32
    ).astype(jnp.bfloat16)
    returned = lax.all_to_all(product, "expert", split_axis=0, concat_axis=0, tiled=True)
    returned_out = returned
    arrived_hidden = received
    expert_terms = returned_out.reshape(group_size * capacity, width)[position].reshape(
        tokens_here, chosen, width
    )
    layer_out = jnp.sum(route_probs[..., None] * expert_terms.astype(jnp.float32), axis=1).astype(
        jnp.bfloat16
    )
    scaled = (route_probs[..., None] * upstream[:, None, :].astype(jnp.float32)).astype(
        jnp.bfloat16
    )
    send_grads = jnp.zeros((group_size * capacity, width), jnp.bfloat16)
    send_grads = send_grads.at[position].set(scaled.reshape(total_rows, width))
    send_grads = send_grads.reshape(group_size, capacity, width)
    received = lax.all_to_all(send_grads, "expert", split_axis=0, concat_axis=0, tiled=True)
    product = jnp.einsum(
        "scd,hd->sch", received, full_weights, preferred_element_type=jnp.float32
    ).astype(jnp.bfloat16)
    returned = lax.all_to_all(product, "expert", split_axis=0, concat_axis=0, tiled=True)
    hidden_grads = returned.reshape(group_size * capacity, hidden_width)[position].reshape(
        tokens_here, chosen, hidden_width
    )
    flat_hidden = arrived_hidden.reshape(group_size * capacity, hidden_width)
    flat_grads = received.reshape(group_size * capacity, width)
    gradient = lax.psum_scatter(
        lax.dot_general(
            flat_hidden, flat_grads, (((0,), (0,)), ((), ())), preferred_element_type=jnp.float32
        ).astype(jnp.bfloat16),
        "dp",
        scatter_dimension=0,
        tiled=True,
    ).astype(jnp.float32)
    new_w, new_first, new_second = adam_update(
        weights_now[0], first_now[0], second_now[0], gradient
    )
    new_w, new_first, new_second = (new_w[None], new_first[None], new_second[None])
    arrived_result = (
        partner(new_w, "expert", top_bit),
        partner(new_first.astype(jnp.bfloat16), "expert", top_bit).astype(new_first.dtype),
        partner(new_second.astype(jnp.bfloat16), "expert", top_bit).astype(new_second.dtype),
    )
    new_w = jnp.where(flip_mine == 1, arrived_result[0], new_w)
    new_first = jnp.where(flip_mine == 1, arrived_result[1], new_first)
    new_second = jnp.where(flip_mine == 1, arrived_result[2], new_second)
    return (layer_out, hidden_grads, new_w, new_first, new_second)


def solution(mesh):
    in_specs = (
        P(("dp", "expert"), None),
        P(("dp", "expert"), None),
        P(("dp", "expert"), None, None),
        P(("dp", "expert"), None),
        P(),
        P(),
        P("expert", "dp", None),
        P("expert", "dp", None),
        P("expert", "dp", None),
    )
    out_specs = (
        P(("dp", "expert"), None),
        P(("dp", "expert"), None, None),
        P("expert", "dp", None),
        P("expert", "dp", None),
        P("expert", "dp", None),
    )
    return jax.shard_map(shards, mesh=mesh, in_specs=in_specs, out_specs=out_specs, check_vma=False)
```

profile of v0, /device:TPU:6, one launch (start us, length us, event | category | flops | bytes accessed | tf_op | source)
XLA Modules:
  0.0 432.4 jit_solution(11244575545764916020)
XLA Ops:
  7.2 0.8 copy.25
  8.1 0.8 select_reduce_fusion.1
  9.4 1.2 scatter_custom_fusion
  10.6 0.8 reshape.75
  11.5 21.4 %all-to-all-start = ((bf16[64,4,768]{2,1,0:T(4,128)(2,1)}), bf16[64,4,768]{2,1,0:T(4,128)(2,1)}, u32[]{:S(2)}, u32[]{:S(2)}) async-start(bf16[64,4,768]{2,1,0:T(4,128)(2,1)} %reshape.75), calls=%async_computation | async-start | bytes 786432 | tf_op jit(solution)/shard_map/all_to_all | solution.py:59
  34.4 0.8 convert_element_type.61
  35.3 1.8 scatter_custom_fusion.1
  37.6 13.9 %all-to-all-done = bf16[64,4,768]{2,1,0:T(4,128)(2,1)} async-done(((bf16[64,4,768]{2,1,0:T(4,128)(2,1)}), bf16[64,4,768]{2,1,0:T(4,128)(2,1)}, u32[]{:S(2)}, u32[]{:S(2)}) %all-to-all-start) | async-done | bytes 393248 | tf_op jit(solution)/shard_map/all_to_all | solution.py:59
  51.4 49.8 %all_to_all.20 = bf16[64,4,2048]{2,1,0:T(4,128)(2,1)S(1)} all-to-all(bf16[64,4,2048]{2,1,0:T(4,128)(2,1)S(1)} %reshape.77), channel_id=1, replica_groups=mesh['dp'=8,'expert'=64] {'expert'}, dimensions={0} | all-to-all | bytes 2097152 | tf_op jit(solution)/shard_map/all_to_all | solution.py:78
  101.3 4.4 %bitcast_convert_fusion = bf16[768,2048]{1,0:T(8,128)(2,1)} fusion(bf16[64,4,2048]{2,1,0:T(4,128)(2,1)S(1)} %all_to_all.20, bf16[64,4,768]{2,1,0:T(4,128)(2,1)} %all-to-all-done), kind=kOutput, calls=%fused_computation.4 | convolution fusion | flops 806879232 | bytes 4587520 | tf_op jit(solution)/shard_map/dot_general | solution.py:89
  105.7 59.7 %all-gather.3.cloned.1.call-done = bf16[1,768,2048]{2,1,0:T(8,128)(2,1)} async-done(((bf16[1,96,2048]{2,1,0:T(8,128)(2,1)}), bf16[1,768,2048]{2,1,0:T(8,128)(2,1)}) %all-gather.3.cloned.1.call-update) | async-done | bytes 3145744 | tf_op jit(solution)/shard_map/all_gather | solution.py:55
  165.4 3.8 fusion.7
  169.3 1.1 copy.30
  170.3 11.9 %all-to-all-start.3 = ((bf16[64,4,768]{2,1,0:T(4,128)(2,1)}), bf16[64,4,768]{2,1,0:T(4,128)(2,1)S(1)}, u32[]{:S(2)}, u32[]{:S(2)}) async-start(bf16[64,4,768]{2,1,0:T(4,128)(2,1)} %copy.30), calls=%async_computation.3 | async-start | bytes 786432 | tf_op jit(solution)/shard_map/all_to_all | solution.py:82
  182.2 3.0 fusion.4
  185.3 1.8 copy.27
  187.1 22.1 %all-to-all-done.3 = bf16[64,4,768]{2,1,0:T(4,128)(2,1)S(1)} async-done(((bf16[64,4,768]{2,1,0:T(4,128)(2,1)}), bf16[64,4,768]{2,1,0:T(4,128)(2,1)S(1)}, u32[]{:S(2)}, u32[]{:S(2)}) %all-to-all-start.3) | async-done | bytes 393248 | tf_op jit(solution)/shard_map/all_to_all | solution.py:82
  209.9 7.0 %all-to-all-start.1 = ((bf16[64,4,2048]{2,1,0:T(4,128)(2,1)}), bf16[64,4,2048]{2,1,0:T(4,128)(2,1)S(1)}, u32[]{:S(2)}, u32[]{:S(2)}) async-start(bf16[64,4,2048]{2,1,0:T(4,128)(2,1)} %copy.27), calls=%async_computation.1 | async-start | bytes 2097152 | tf_op jit(solution)/shard_map/all_to_all | solution.py:63
  216.9 92.8 %reduce-scatter.2.cloned.1.call-done = bf16[96,2048]{1,0:T(8,128)(2,1)} async-done(((bf16[768,2048]{1,0:T(8,128)(2,1)}), bf16[96,2048]{1,0:T(8,128)(2,1)}) %reduce-scatter.2.cloned.1.call-update) | async-done | bytes 393232 | tf_op jit(solution)/shard_map/reduce_scatter | solution.py:88
  309.8 2.8 convert_bitcast_fusion
  312.6 5.6 %collective-permute-start = (bf16[1,96,2048]{2,1,0:T(8,128)(2,1)}, bf16[1,96,2048]{2,1,0:T(8,128)(2,1)}, u32[]{:S(2)}, u32[]{:S(2)}) collective-permute-start(bf16[1,96,2048]{2,1,0:T(8,128)(2,1)} %get-tuple-element.6), channel_id=1, source_target_pairs={{0,32},{32,0},{1,33},{33,1},{2,34},{34,2},{3,35},{35,3},{4,36},{36... | collective-permute-start | bytes 1179656 | tf_op jit(solution)/shard_map/ppermute | solution.py:21
  319.5 1.1 reshape.78
  320.6 1.5 gather_fusion.1
  322.4 1.7 gather_fusion
  324.1 2.1 fusion.10
  326.3 8.9 %collective-permute-start.2 = (bf16[1,96,2048]{2,1,0:T(8,128)(2,1)}, bf16[1,96,2048]{2,1,0:T(8,128)(2,1)S(1)}, u32[]{:S(2)}, u32[]{:S(2)}) collective-permute-start(bf16[1,96,2048]{2,1,0:T(8,128)(2,1)} %get-tuple-element.5), channel_id=1, source_target_pairs={{0,32},{32,0},{1,33},{33,1},{2,34},{34,2},{3,35},{35,3},{4,36},{36... | collective-permute-start | bytes 1179656 | tf_op jit(solution)/shard_map/ppermute | solution.py:21
  335.2 5.6 %collective-permute-start.1 = (bf16[1,96,2048]{2,1,0:T(8,128)(2,1)}, bf16[1,96,2048]{2,1,0:T(8,128)(2,1)S(1)}, u32[]{:S(2)}, u32[]{:S(2)}) collective-permute-start(bf16[1,96,2048]{2,1,0:T(8,128)(2,1)} %get-tuple-element.7), channel_id=1, source_target_pairs={{0,32},{32,0},{1,33},{33,1},{2,34},{34,2},{3,35},{35,3},{4,36},{36... | collective-permute-start | bytes 1179656 | tf_op jit(solution)/shard_map/ppermute | solution.py:21
  340.8 66.6 %collective-permute-done = bf16[1,96,2048]{2,1,0:T(8,128)(2,1)} collective-permute-done((bf16[1,96,2048]{2,1,0:T(8,128)(2,1)}, bf16[1,96,2048]{2,1,0:T(8,128)(2,1)}, u32[]{:S(2)}, u32[]{:S(2)}) %collective-permute-start) | collective-permute-done | bytes 393248 | tf_op jit(solution)/shard_map/ppermute | solution.py:21
  407.4 1.8 broadcast_select_fusion
  409.2 6.5 %collective-permute-done.2 = bf16[1,96,2048]{2,1,0:T(8,128)(2,1)S(1)} collective-permute-done((bf16[1,96,2048]{2,1,0:T(8,128)(2,1)}, bf16[1,96,2048]{2,1,0:T(8,128)(2,1)S(1)}, u32[]{:S(2)}, u32[]{:S(2)}) %collective-permute-start.2) | collective-permute-done | bytes 393248 | tf_op jit(solution)/shard_map/ppermute | solution.py:21
  415.8 8.3 %collective-permute-done.1 = bf16[1,96,2048]{2,1,0:T(8,128)(2,1)S(1)} collective-permute-done((bf16[1,96,2048]{2,1,0:T(8,128)(2,1)}, bf16[1,96,2048]{2,1,0:T(8,128)(2,1)S(1)}, u32[]{:S(2)}, u32[]{:S(2)}) %collective-permute-start.1) | collective-permute-done | bytes 393248 | tf_op jit(solution)/shard_map/ppermute | solution.py:21
  424.1 1.5 bitcast_select_fusion
  (32 shorter events, 4.3 us)
Async XLA Ops:
  7.2 2.2 copy-start
  11.5 40.0 %all-to-all-start = ((bf16[64,4,768]{2,1,0:T(4,128)(2,1)}), bf16[64,4,768]{2,1,0:T(4,128)(2,1)}, u32[]{:S(2)}, u32[]{:S(2)}) async-start(bf16[64,4,768]{2,1,0:T(4,128)(2,1)} %reshape.75), calls=%async_computation | async-start | bytes 786432 | tf_op jit(solution)/shard_map/all_to_all | solution.py:59
  32.9 132.5 %all-gather.3.cloned.1.call-start = ((), (), s32[]{:S(2)}) async-start(), calls=%async_computation.6 | async-start | bytes 3538944 | tf_op jit(solution)/shard_map/all_gather | solution.py:55
  33.6 276.2 %reduce-scatter.2.cloned.1.call-start = ((), (), s32[]{:S(2)}) async-start(), calls=%async_computation.5 | async-start | bytes 3538944 | tf_op jit(solution)/shard_map/reduce_scatter | solution.py:88
  170.3 38.9 %all-to-all-start.3 = ((bf16[64,4,768]{2,1,0:T(4,128)(2,1)}), bf16[64,4,768]{2,1,0:T(4,128)(2,1)S(1)}, u32[]{:S(2)}, u32[]{:S(2)}) async-start(bf16[64,4,768]{2,1,0:T(4,128)(2,1)} %copy.30), calls=%async_computation.3 | async-start | bytes 786432 | tf_op jit(solution)/shard_map/all_to_all | solution.py:82
  185.2 124.5 %copy-start.1 = (f32[1,96,2048]{2,1,0:T(8,128)S(1)}, f32[1,96,2048]{2,1,0:T(8,128)}, u32[]{:S(2)}) copy-start(f32[1,96,2048]{2,1,0:T(8,128)} %param.17) | copy-start | bytes 2359300
  185.3 124.5 %copy-start.2 = (f32[1,96,2048]{2,1,0:T(8,128)S(1)}, f32[1,96,2048]{2,1,0:T(8,128)}, u32[]{:S(2)}) copy-start(f32[1,96,2048]{2,1,0:T(8,128)} %param.16) | copy-start | bytes 2359300
  185.3 124.5 %copy-start.5 = (bf16[1,96,2048]{2,1,0:T(8,128)(2,1)S(1)}, bf16[1,96,2048]{2,1,0:T(8,128)(2,1)}, u32[]{:S(2)}) copy-start(bf16[1,96,2048]{2,1,0:T(8,128)(2,1)} %param.15) | copy-start | bytes 1179652
  187.1 131.1 %copy-start.7 = (s32[64]{0:T(128)S(1)}, s32[64]{0:T(128)}, u32[]{:S(2)}) copy-start(s32[64]{0:T(128)} %param.14) | copy-start | bytes 772
  209.2 0.7 copy-start.6
  209.9 112.2 %all-to-all-start.1 = ((bf16[64,4,2048]{2,1,0:T(4,128)(2,1)}), bf16[64,4,2048]{2,1,0:T(4,128)(2,1)S(1)}, u32[]{:S(2)}, u32[]{:S(2)}) async-start(bf16[64,4,2048]{2,1,0:T(4,128)(2,1)} %copy.27), calls=%async_computation.1 | async-start | bytes 2097152 | tf_op jit(solution)/shard_map/all_to_all | solution.py:63
  312.6 94.9 %collective-permute-start = (bf16[1,96,2048]{2,1,0:T(8,128)(2,1)}, bf16[1,96,2048]{2,1,0:T(8,128)(2,1)}, u32[]{:S(2)}, u32[]{:S(2)}) collective-permute-start(bf16[1,96,2048]{2,1,0:T(8,128)(2,1)} %get-tuple-element.6), channel_id=1, source_target_pairs={{0,32},{32,0},{1,33},{33,1},{2,34},{34,2},{3,35},{35,3},{4,36},{36... | collective-permute-start | bytes 1179656 | tf_op jit(solution)/shard_map/ppermute | solution.py:21
  322.4 101.7 %copy-start.3 = (f32[1,96,2048]{2,1,0:T(8,128)S(1)}, f32[1,96,2048]{2,1,0:T(8,128)}, u32[]{:S(2)}) copy-start(f32[1,96,2048]{2,1,0:T(8,128)} %param.16) | copy-start | bytes 2359300
  322.4 101.7 %copy-start.4 = (bf16[96,2048]{1,0:T(8,128)(2,1)S(1)}, bf16[96,2048]{1,0:T(8,128)(2,1)}, u32[]{:S(2)}) copy-start(bf16[96,2048]{1,0:T(8,128)(2,1)} %reduce-scatter.2.cloned.1.call-done) | copy-start | bytes 1179652
  326.3 89.5 %collective-permute-start.2 = (bf16[1,96,2048]{2,1,0:T(8,128)(2,1)}, bf16[1,96,2048]{2,1,0:T(8,128)(2,1)S(1)}, u32[]{:S(2)}, u32[]{:S(2)}) collective-permute-start(bf16[1,96,2048]{2,1,0:T(8,128)(2,1)} %get-tuple-element.5), channel_id=1, source_target_pairs={{0,32},{32,0},{1,33},{33,1},{2,34},{34,2},{3,35},{35,3},{4,36},{36... | collective-permute-start | bytes 1179656 | tf_op jit(solution)/shard_map/ppermute | solution.py:21
  335.2 88.9 %collective-permute-start.1 = (bf16[1,96,2048]{2,1,0:T(8,128)(2,1)}, bf16[1,96,2048]{2,1,0:T(8,128)(2,1)S(1)}, u32[]{:S(2)}, u32[]{:S(2)}) collective-permute-start(bf16[1,96,2048]{2,1,0:T(8,128)(2,1)} %get-tuple-element.7), channel_id=1, source_target_pairs={{0,32},{32,0},{1,33},{33,1},{2,34},{34,2},{3,35},{35,3},{4,36},{36... | collective-permute-start | bytes 1179656 | tf_op jit(solution)/shard_map/ppermute | solution.py:21
Sparse Core Ops, SparseCore 0:
  35.8 129.5 all-gather.2
  168.2 141.4 reduce-scatter.1
where the time goes:
time: 434 us; the launch traced here: 432 us
  waiting for transfers between devices  271 us (62%)
  starting transfers between devices  60.5 us (14%)
  blocking collectives  49.8 us (11%)
  between operations  14.9 us (3%)
  other arithmetic  12.7 us (3%)
  local copies, waits for them, and re-layouts  12.5 us (3%)
  matrix products  11.3 us (3%)
    reduce_scatter x1, waiting for transfers between devices, shards(): lax.psum_scatter(lax.dot_general(flat_hidden, flat_grads, (((0,), (0,)),...  92.8 us
    ppermute x3, waiting for transfers between devices, partner(): return lax.ppermute(block, axis, route)  81.5 us
    all_gather x1, waiting for transfers between devices, shards(): full_weights = lax.all_gather(weights_now[0], 'dp', axis=0, tiled=True)  59.7 us
    all_to_all x1, blocking collectives, shards(): lax.all_to_all(send_grads, 'expert', split_axis=0, concat_axis=0, tiled=T...  49.8 us
    all_to_all x2, waiting for transfers between devices, shards(): lax.all_to_all(product, 'expert', split_axis=0, concat_axis=0, tiled=True)  22.1 us
    all_to_all x1, starting transfers between devices, shards(): lax.all_to_all(send_hidden, 'expert', split_axis=0, concat_axis=0, tiled=...  21.4 us
    ppermute x3, starting transfers between devices, partner(): return lax.ppermute(block, axis, route)  20.1 us
    all_to_all x2, starting transfers between devices, shards(): lax.all_to_all(product, 'expert', split_axis=0, concat_axis=0, tiled=True)  18.9 us
  transfers between devices with their start and end apart: 8, of which 7 were waited for; matrix products, arithmetic and copies ran while one was open for 7% of the time, Pallas kernels for 0%

commit v1 on v0

v1 whole, which is shorter than its diff:
```python
import jax
import jax.numpy as jnp
from jax import lax
from jax.sharding import Mesh, PartitionSpec as P

decay_one = 0.9
decay_two = 0.95
learn_rate = 0.01
bias_one = 1.0 - 0.9**10
bias_two = 1.0 - 0.95**10
epsilon = 1e-08


def adam_update(weight, first, second, gradient):
    new_first = decay_one * first + (1.0 - decay_one) * gradient
    new_second = decay_two * second + (1.0 - decay_two) * gradient * gradient
    step_size = learn_rate * (new_first / bias_one) / (jnp.sqrt(new_second / bias_two) + epsilon)
    return ((weight.astype(jnp.float32) - step_size).astype(jnp.bfloat16), new_first, new_second)


def table_lookup(lookup_table, positions):
    iota_slots = jnp.arange(lookup_table.shape[0], dtype=jnp.int32)
    matches = positions[..., None] == iota_slots
    return jnp.sum(jnp.where(matches, lookup_table, 0), axis=-1)


def shards(
    route_ids, route_probs, hidden, upstream, placement, swap_flags, weights, moment1, moment2
):
    plane = lax.axis_size("p")
    my_half, my_place, my_dp = lax.axis_index("zh"), lax.axis_index("p"), lax.axis_index("dp")
    tokens_here, chosen = route_ids.shape
    width = upstream.shape[1]
    hidden_width = hidden.shape[2]
    rows_dp = weights.shape[1]
    total_rows = tokens_here * chosen
    capacity = total_rows // plane
    slots = 2 * capacity
    flip_mine = table_lookup(swap_flags, my_place)

    across = [(0, 1), (1, 0)]
    first_far = lax.ppermute(moment1.astype(jnp.bfloat16), "zh", across)
    second_far = lax.ppermute(moment2.astype(jnp.bfloat16), "zh", across)
    full_weights = lax.all_gather(weights[0], ("zh", "dp"), axis=0, tiled=True)

    target = table_lookup(placement, route_ids.reshape(-1))
    slot_iota = jnp.arange(2 * plane, dtype=jnp.int32)
    onehot = (target[:, None] == slot_iota[None, :]).astype(jnp.int32)
    rank = jnp.sum((jnp.cumsum(onehot, axis=0) - onehot) * onehot, axis=1)
    position = (target % plane) * slots + (target // plane) * capacity + rank

    send_hidden = jnp.zeros((plane * slots, hidden_width), jnp.bfloat16)
    send_hidden = send_hidden.at[position].set(hidden.reshape(total_rows, hidden_width))
    send_hidden = send_hidden.reshape(plane, slots, hidden_width)
    got_hidden = lax.all_to_all(send_hidden, "p", split_axis=0, concat_axis=0, tiled=True)
    scaled = (route_probs[..., None] * upstream[:, None, :].astype(jnp.float32)).astype(
        jnp.bfloat16
    )
    send_grads = jnp.zeros((plane * slots, width), jnp.bfloat16)
    send_grads = send_grads.at[position].set(scaled.reshape(total_rows, width))
    send_grads = send_grads.reshape(plane, slots, width)
    got_grads = lax.all_to_all(send_grads, "p", split_axis=0, concat_axis=0, tiled=True)

    flat_hidden = got_hidden.reshape(plane * slots, hidden_width)
    flat_grads = got_grads.reshape(plane * slots, width)
    half = (jnp.arange(plane * slots, dtype=jnp.int32) // capacity % 2)[:, None]
    zero = jnp.zeros_like(flat_hidden)
    spread = jnp.concatenate(
        [jnp.where(half == 0, flat_hidden, zero), jnp.where(half == 1, flat_hidden, zero)], axis=1
    )
    new_half = half ^ flip_mine
    spread_new = jnp.concatenate(
        [jnp.where(new_half == 0, flat_hidden, zero), jnp.where(new_half == 1, flat_hidden, zero)],
        axis=1,
    )
    partial = lax.dot_general(
        spread_new, flat_grads, (((0,), (0,)), ((), ())), preferred_element_type=jnp.float32
    ).astype(jnp.bfloat16)
    gradient = lax.psum_scatter(
        partial, ("zh", "dp"), scatter_dimension=0, tiled=True
    ).astype(jnp.float32)

    terms = jnp.dot(spread, full_weights, preferred_element_type=jnp.float32).astype(jnp.bfloat16)
    back_terms = lax.all_to_all(
        terms.reshape(plane, slots, width), "p", split_axis=0, concat_axis=0, tiled=True
    )
    both = lax.dot_general(
        flat_grads, full_weights, (((1,), (1,)), ((), ())), preferred_element_type=jnp.float32
    ).astype(jnp.bfloat16)
    row_grads = jnp.where(half == 0, both[:, :hidden_width], both[:, hidden_width:])
    back_grads = lax.all_to_all(
        row_grads.reshape(plane, slots, hidden_width), "p", split_axis=0, concat_axis=0, tiled=True
    )
    expert_terms = back_terms.reshape(plane * slots, width)[position].reshape(
        tokens_here, chosen, width
    )
    layer_out = jnp.sum(route_probs[..., None] * expert_terms.astype(jnp.float32), axis=1).astype(
        jnp.bfloat16
    )
    hidden_grads = back_grads.reshape(plane * slots, hidden_width)[position].reshape(
        tokens_here, chosen, hidden_width
    )

    old_half = my_half ^ flip_mine
    weight_here = lax.dynamic_slice_in_dim(
        full_weights, old_half * hidden_width + my_dp * rows_dp, rows_dp, 0
    )
    first_here = jnp.where(flip_mine == 1, first_far[0].astype(jnp.float32), moment1[0])
    second_here = jnp.where(flip_mine == 1, second_far[0].astype(jnp.float32), moment2[0])
    new_w, new_first, new_second = adam_update(weight_here, first_here, second_here, gradient)
    return (layer_out, hidden_grads, new_w[None], new_first[None], new_second[None])


def solution(mesh):
    n_dp, n_expert = mesh.shape["dp"], mesh.shape["expert"]
    mesh = Mesh(mesh.devices.reshape(n_dp, 2, n_expert // 2), ("dp", "zh", "p"))
    tokens, experts = ("dp", "zh", "p"), ("zh", "p")
    in_specs = (
        P(tokens, None),
        P(tokens, None),
        P(tokens, None, None),
        P(tokens, None),
        P(),
        P(),
        P(experts, "dp", None),
        P(experts, "dp", None),
        P(experts, "dp", None),
    )
    out_specs = (
        P(tokens, None),
        P(tokens, None, None),
        P(experts, "dp", None),
        P(experts, "dp", None),
        P(experts, "dp", None),
    )
    return jax.shard_map(shards, mesh=mesh, in_specs=in_specs, out_specs=out_specs, check_vma=False)
```

time: 434 us -> 273 us (0.63)
  waiting for transfers between devices: 271 us -> 176 us
  blocking collectives: 49.8 us -> 0 us
  starting transfers between devices: 60.5 us -> 44.1 us
  local copies, waits for them, and re-layouts: 12.5 us -> 6.85 us
    reduce_scatter x1, waiting for transfers between devices: 92.8 us -> 31.6 us  [shards(): lax.psum_scatter(partial, ('zh', 'dp'), scatter_dimension=0, tiled=True)]
    all_to_all x1 -> x0, blocking collectives: 49.8 us -> none  [shards(): lax.all_to_all(send_grads, 'expert', split_axis=0, concat_axis=0, tiled=T...]
    all_to_all x3 -> x4, waiting for transfers between devices: 36 us -> 13.2 us  [the longest x1 10.9 us: shards(): lax.all_to_all(send_grads, 'p', split_axis=0, concat_axis=0, tiled=True)]
    all_to_all x3 -> x4, starting transfers between devices: 40.3 us -> 29.5 us  [the longest x1 9.46 us: shards(): lax.all_to_all(send_grads, 'p', split_axis=0, concat_axis=0, tiled=True)]
    ppermute x3 -> x2, waiting for transfers between devices: 81.5 us -> 75.1 us  [the longest x1 41.5 us: shards(): first_far = lax.ppermute(moment1.astype(jnp.bfloat16), 'zh', across)]
    ppermute x3 -> x2, starting transfers between devices: 20.1 us -> 14.5 us  [the longest x1 8.14 us: shards(): second_far = lax.ppermute(moment2.astype(jnp.bfloat16), 'zh', across)]
  transfers between devices with their start and end apart: 8 -> 8, of which waited for: 7 -> 6; matrix products, arithmetic and copies ran while one was open for 7% -> 10% of each run, Pallas kernels for 0% -> 0%
where the time goes in v1:
time: 273 us; the launch traced here: 272 us
  waiting for transfers between devices  176 us (64%)
  starting transfers between devices  44.1 us (16%)
  between operations  15.5 us (6%)
  matrix products  14.8 us (5%)
  other arithmetic  14.6 us (5%)
  local copies, waits for them, and re-layouts  6.85 us (3%)
    all_gather x1, waiting for transfers between devices, shards(): full_weights = lax.all_gather(weights[0], ('zh', 'dp'), axis=0, tiled=True)  55.6 us
    ppermute x1, waiting for transfers between devices, shards(): first_far = lax.ppermute(moment1.astype(jnp.bfloat16), 'zh', across)  41.5 us
    ppermute x1, waiting for transfers between devices, shards(): second_far = lax.ppermute(moment2.astype(jnp.bfloat16), 'zh', across)  33.6 us
    reduce_scatter x1, waiting for transfers between devices, shards(): lax.psum_scatter(partial, ('zh', 'dp'), scatter_dimension=0, tiled=True)  31.6 us
    all_to_all x1, waiting for transfers between devices, shards(): lax.all_to_all(send_grads, 'p', split_axis=0, concat_axis=0, tiled=True)  10.9 us
    all_to_all x1, starting transfers between devices, shards(): lax.all_to_all(send_grads, 'p', split_axis=0, concat_axis=0, tiled=True)  9.46 us
    ppermute x1, starting transfers between devices, shards(): second_far = lax.ppermute(moment2.astype(jnp.bfloat16), 'zh', across)  8.14 us
    all_to_all x1, starting transfers between devices, shards(): lax.all_to_all(row_grads.reshape(plane, slots, hidden_width), 'p', split_...  7.42 us
  transfers between devices with their start and end apart: 8, of which 6 were waited for; matrix products, arithmetic and copies ran while one was open for 10% of the time, Pallas kernels for 0%

profile of v1, /device:TPU:6, one launch (start us, length us, event | category | flops | bytes accessed | tf_op | source)
XLA Modules:
  0.0 272.1 jit_solution(17750998159652108465)
XLA Ops:
  7.2 0.7 all-gather.3.cloned.1.call-update
  7.9 0.8 copy.18
  8.8 0.9 convert_element_type.57
  9.6 0.8 copy.17
  10.5 0.8 select_reduce_fusion.1
  11.4 0.2 reduce_window_sum.11
  11.8 2.5 scatter_custom_fusion.1
  14.3 9.5 %all-to-all-start.2 = ((bf16[32,8,2048]{2,1,0:T(8,128)(2,1)}), bf16[32,8,2048]{2,1,0:T(8,128)(2,1)S(1)}, u32[]{:S(2)}, u32[]{:S(2)}) async-start(bf16[32,8,2048]{2,1,0:T(8,128)(2,1)} %bitcast.11), calls=%async_computation.2 | async-start | bytes 2097152 | tf_op jit(solution)/shard_map/all_to_all | solution.py:62
  23.8 1.9 scatter_custom_fusion
  25.7 1.3 fusion.43
  27.0 0.7 xor_compare_fusion
  27.6 10.9 %all-to-all-done.2 = bf16[32,8,2048]{2,1,0:T(8,128)(2,1)S(1)} async-done(((bf16[32,8,2048]{2,1,0:T(8,128)(2,1)}), bf16[32,8,2048]{2,1,0:T(8,128)(2,1)S(1)}, u32[]{:S(2)}, u32[]{:S(2)}) %all-to-all-start.2) | async-done | bytes 1048608 | tf_op jit(solution)/shard_map/all_to_all | solution.py:62
  38.5 6.5 %all-to-all-start = ((bf16[32,8,768]{2,1,0:T(8,128)(2,1)}), bf16[32,8,768]{2,1,0:T(8,128)(2,1)S(1)}, u32[]{:S(2)}, u32[]{:S(2)}) async-start(bf16[32,8,768]{2,1,0:T(8,128)(2,1)} %bitcast.4), calls=%async_computation | async-start | bytes 786432 | tf_op jit(solution)/shard_map/all_to_all | solution.py:55
  45.0 55.6 %all-gather.3.cloned.1.call-done = bf16[1,1536,2048]{2,1,0:T(8,128)(2,1)} async-done(((bf16[1,96,2048]{2,1,0:T(8,128)(2,1)}), bf16[1,1536,2048]{2,1,0:T(8,128)(2,1)}) %all-gather.3.cloned.1.call-update) | async-done | bytes 6291472 | tf_op jit(solution)/shard_map/all_gather | solution.py:44
  100.7 4.6 %fusion.7 = bf16[256,1536]{1,0:T(8,128)(2,1)S(1)} fusion(bf16[1,1536,2048]{2,1,0:T(8,128)(2,1)} %all-gather.3.cloned.1.call-done, bf16[32,8,2048]{2,1,0:T(8,128)(2,1)S(1)} %all-to-all-done.2), kind=kOutput, calls=%fused_computation.10 | convolution fusion | flops 1611005952 | bytes 8126464 | tf_op jit(solution)/shard_map/dot_general | solution.py:87
  105.3 0.9 bitcast_select_fusion.1
  106.2 4.5 %convolution_convert_fusion = bf16[1536,2048]{1,0:T(8,128)(2,1)} fusion(bf16[32,8,2048]{2,1,0:T(8,128)(2,1)S(1)} %all-to-all-done.2, bf16[256,768]{1,0:T(8,128)(2,1)S(1)} %get-tuple-element.10, bf16[256,768]{1,0:T(8,128)(2,1)S(1)} %get-tuple-element.8), kind=kOutput, calls=%fused_computation.4 | convolution fusion | flops 1615331328 | bytes 8126464 | tf_op jit(solution)/shard_map/dot_general | solution.py:76
  110.8 7.4 %all-to-all-start.3 = ((bf16[32,8,768]{2,1,0:T(8,128)(2,1)}), bf16[32,8,768]{2,1,0:T(8,128)(2,1)S(1)}, u32[]{:S(2)}, u32[]{:S(2)}) async-start(bf16[32,8,768]{2,1,0:T(8,128)(2,1)} %get-tuple-element.12), calls=%async_computation.3 | async-start | bytes 786432 | tf_op jit(solution)/shard_map/all_to_all | solution.py:91
  118.2 5.7 %fusion.10 = bf16[32,8,2048]{2,1,0:T(8,128)(2,1)} fusion(bf16[1,1536,2048]{2,1,0:T(8,128)(2,1)} %all-gather.3.cloned.1.call-done, bf16[256,768]{1,0:T(8,128)(2,1)S(1)} %get-tuple-element.9, bf16[256,768]{1,0:T(8,128)(2,1)S(1)} %get-tuple-element.11), kind=kOutput, calls=%fused_computation.11 | convolution fusion | flops 1612709888 | bytes 8126464 | tf_op jit(solution)/shard_map/dot_general | solution.py:83
  124.0 2.3 all-to-all-done.3
  126.3 6.1 %all-to-all-start.1 = ((bf16[32,8,2048]{2,1,0:T(8,128)(2,1)}), bf16[32,8,2048]{2,1,0:T(8,128)(2,1)S(1)}, u32[]{:S(2)}, u32[]{:S(2)}) async-start(bf16[32,8,2048]{2,1,0:T(8,128)(2,1)} %fusion.10), calls=%async_computation.1 | async-start | bytes 2097152 | tf_op jit(solution)/shard_map/all_to_all | solution.py:84
  132.4 0.8 convert_element_type.65
  133.2 8.1 %collective-permute-start.1 = (bf16[1,96,2048]{2,1,0:T(8,128)(2,1)}, bf16[1,96,2048]{2,1,0:T(8,128)(2,1)}, u32[]{:S(2)}, u32[]{:S(2)}) collective-permute-start(bf16[1,96,2048]{2,1,0:T(8,128)(2,1)} %convert_element_type.65), channel_id=1, source_target_pairs={{0,32},{32,0},{1,33},{33,1},{2,34},{34,2},{3,35},{35,3},{4,36},{36... | collective-permute-start | bytes 1179656 | tf_op jit(solution)/shard_map/ppermute | solution.py:43
  141.3 0.8 convert_element_type.61
  142.1 6.4 %collective-permute-start = (bf16[1,96,2048]{2,1,0:T(8,128)(2,1)}, bf16[1,96,2048]{2,1,0:T(8,128)(2,1)}, u32[]{:S(2)}, u32[]{:S(2)}) collective-permute-start(bf16[1,96,2048]{2,1,0:T(8,128)(2,1)} %convert_element_type.61), channel_id=1, source_target_pairs={{0,32},{32,0},{1,33},{33,1},{2,34},{34,2},{3,35},{35,3},{4,36},{36... | collective-permute-start | bytes 1179656 | tf_op jit(solution)/shard_map/ppermute | solution.py:42
  149.8 1.5 gather_fusion.1
  151.4 1.7 gather_fusion
  153.1 2.1 fusion.13
  155.2 33.6 %collective-permute-done.1 = bf16[1,96,2048]{2,1,0:T(8,128)(2,1)} collective-permute-done((bf16[1,96,2048]{2,1,0:T(8,128)(2,1)}, bf16[1,96,2048]{2,1,0:T(8,128)(2,1)}, u32[]{:S(2)}, u32[]{:S(2)}) %collective-permute-start.1) | collective-permute-done | bytes 393248 | tf_op jit(solution)/shard_map/ppermute | solution.py:43
  188.8 41.5 %collective-permute-done = bf16[1,96,2048]{2,1,0:T(8,128)(2,1)} collective-permute-done((bf16[1,96,2048]{2,1,0:T(8,128)(2,1)}, bf16[1,96,2048]{2,1,0:T(8,128)(2,1)}, u32[]{:S(2)}, u32[]{:S(2)}) %collective-permute-start) | collective-permute-done | bytes 393248 | tf_op jit(solution)/shard_map/ppermute | solution.py:42
  230.3 31.6 %reduce-scatter.2.cloned.1.call-done = bf16[96,2048]{1,0:T(8,128)(2,1)} async-done(((bf16[1536,2048]{1,0:T(8,128)(2,1)}), bf16[96,2048]{1,0:T(8,128)(2,1)}) %reduce-scatter.2.cloned.1.call-update) | async-done | bytes 393232 | tf_op jit(solution)/shard_map/reduce_scatter | solution.py:79
  261.9 3.3 %fusion.37 = (f32[1,96,2048]{2,1,0:T(8,128)}, bf16[1,96,2048]{2,1,0:T(8,128)(2,1)}, f32[1,96,2048]{2,1,0:T(8,128)}) fusion(bf16[96,2048]{1,0:T(8,128)(2,1)} %reduce-scatter.2.cloned.1.call-done, f32[1,96,2048]{2,1,0:T(8,128)S(1)} %copy-done.1, bf16[1,96,2048]{2,1,0:T(8,128)(2,1)} %collective-permute-done.1, pred[]{:T(512)S(6)} %eq.90, ...), kind=kLoop, calls=%fused_computation.45 | loop fusion | flops 3735552 | bytes 5111813 | tf_op jit(solution)/shard_map/broadcast_in_dim | solution.py:111
  (18 shorter events, 0.6 us)
Async XLA Ops:
  7.2 16.6 %copy-start = (bf16[16,8,768]{2,1,0:T(8,128)(2,1)S(1)}, bf16[16,8,768]{2,1,0:T(8,128)(2,1)}, u32[]{:S(2)}) copy-start(bf16[16,8,768]{2,1,0:T(8,128)(2,1)} %param.11) | copy-start | bytes 589828
  7.2 93.5 %all-gather.3.cloned.1.call-start = ((), (), s32[]{:S(2)}) async-start(), calls=%async_computation.6 | async-start | bytes 6684672 | tf_op jit(solution)/shard_map/all_gather | solution.py:44
  14.3 24.2 %all-to-all-start.2 = ((bf16[32,8,2048]{2,1,0:T(8,128)(2,1)}), bf16[32,8,2048]{2,1,0:T(8,128)(2,1)S(1)}, u32[]{:S(2)}, u32[]{:S(2)}) async-start(bf16[32,8,2048]{2,1,0:T(8,128)(2,1)} %bitcast.11), calls=%async_computation.2 | async-start | bytes 2097152 | tf_op jit(solution)/shard_map/all_to_all | solution.py:62
  38.5 66.8 %all-to-all-start = ((bf16[32,8,768]{2,1,0:T(8,128)(2,1)}), bf16[32,8,768]{2,1,0:T(8,128)(2,1)S(1)}, u32[]{:S(2)}, u32[]{:S(2)}) async-start(bf16[32,8,768]{2,1,0:T(8,128)(2,1)} %bitcast.4), calls=%async_computation | async-start | bytes 786432 | tf_op jit(solution)/shard_map/all_to_all | solution.py:55
  45.0 216.9 %reduce-scatter.2.cloned.1.call-start = ((), (), s32[]{:S(2)}) async-start(), calls=%async_computation.5 | async-start | bytes 6684672 | tf_op jit(solution)/shard_map/reduce_scatter | solution.py:79
  110.8 15.5 %all-to-all-start.3 = ((bf16[32,8,768]{2,1,0:T(8,128)(2,1)}), bf16[32,8,768]{2,1,0:T(8,128)(2,1)S(1)}, u32[]{:S(2)}, u32[]{:S(2)}) async-start(bf16[32,8,768]{2,1,0:T(8,128)(2,1)} %get-tuple-element.12), calls=%async_computation.3 | async-start | bytes 786432 | tf_op jit(solution)/shard_map/all_to_all | solution.py:91
  118.2 14.2 %copy-start.1 = (f32[1,96,2048]{2,1,0:T(8,128)S(1)}, f32[1,96,2048]{2,1,0:T(8,128)}, u32[]{:S(2)}) copy-start(f32[1,96,2048]{2,1,0:T(8,128)} %param.17) | copy-start | bytes 2359300
  118.2 23.1 %copy-start.2 = (f32[1,96,2048]{2,1,0:T(8,128)S(1)}, f32[1,96,2048]{2,1,0:T(8,128)}, u32[]{:S(2)}) copy-start(f32[1,96,2048]{2,1,0:T(8,128)} %param.16) | copy-start | bytes 2359300
  126.3 25.1 %all-to-all-start.1 = ((bf16[32,8,2048]{2,1,0:T(8,128)(2,1)}), bf16[32,8,2048]{2,1,0:T(8,128)(2,1)S(1)}, u32[]{:S(2)}, u32[]{:S(2)}) async-start(bf16[32,8,2048]{2,1,0:T(8,128)(2,1)} %fusion.10), calls=%async_computation.1 | async-start | bytes 2097152 | tf_op jit(solution)/shard_map/all_to_all | solution.py:84
  133.2 55.7 %collective-permute-start.1 = (bf16[1,96,2048]{2,1,0:T(8,128)(2,1)}, bf16[1,96,2048]{2,1,0:T(8,128)(2,1)}, u32[]{:S(2)}, u32[]{:S(2)}) collective-permute-start(bf16[1,96,2048]{2,1,0:T(8,128)(2,1)} %convert_element_type.65), channel_id=1, source_target_pairs={{0,32},{32,0},{1,33},{33,1},{2,34},{34,2},{3,35},{35,3},{4,36},{36... | collective-permute-start | bytes 1179656 | tf_op jit(solution)/shard_map/ppermute | solution.py:43
  142.1 88.2 %collective-permute-start = (bf16[1,96,2048]{2,1,0:T(8,128)(2,1)}, bf16[1,96,2048]{2,1,0:T(8,128)(2,1)}, u32[]{:S(2)}, u32[]{:S(2)}) collective-permute-start(bf16[1,96,2048]{2,1,0:T(8,128)(2,1)} %convert_element_type.61), channel_id=1, source_target_pairs={{0,32},{32,0},{1,33},{33,1},{2,34},{34,2},{3,35},{35,3},{4,36},{36... | collective-permute-start | bytes 1179656 | tf_op jit(solution)/shard_map/ppermute | solution.py:42
Sparse Core Ops, SparseCore 0:
  10.1 90.5 all-gather.2
  110.9 150.9 reduce-scatter.1

commit v2 on v1

--- a/solution.py
+++ b/solution.py
@@ -1,6 +1,8 @@
 import jax
 import jax.numpy as jnp
 from jax import lax
+from jax.experimental import pallas as pl
+from jax.experimental.pallas import tpu as pltpu
 from jax.sharding import Mesh, PartitionSpec as P
 
 decay_one = 0.9
@@ -11,11 +13,76 @@
 epsilon = 1e-08
 
 
+LANES, STEP = 128, 4
+
+
 def adam_update(weight, first, second, gradient):
     new_first = decay_one * first + (1.0 - decay_one) * gradient
     new_second = decay_two * second + (1.0 - decay_two) * gradient * gradient
     step_size = learn_rate * (new_first / bias_one) / (jnp.sqrt(new_second / bias_two) + epsilon)
     return ((weight.astype(jnp.float32) - step_size).astype(jnp.bfloat16), new_first, new_second)
+
+
+def pack_kernel(first_ref, second_ref, out_ref):
+    for block in range(out_ref.shape[1]):
+        columns = pl.ds(block * LANES, LANES)
+        out_ref[0, block] = first_ref[0, :, columns].astype(jnp.bfloat16)
+        out_ref[1, block] = second_ref[0, :, columns].astype(jnp.bfloat16)
+
+
+def pack_moments(first, second):
+    _, rows, width = first.shape
+    blocks = width // LANES
+    step = STEP if blocks % STEP == 0 else 1
+    moment = pl.BlockSpec((1, rows, step * LANES), lambda i: (0, 0, i))
+    return pl.pallas_call(
+        pack_kernel,
+        grid=(blocks // step,),
+        in_specs=[moment, moment],
+        out_specs=pl.BlockSpec((2, step, rows, LANES), lambda i: (0, i, 0, 0)),
+        out_shape=jax.ShapeDtypeStruct((2, blocks, rows, LANES), jnp.bfloat16),
+    )(first, second)
+
+
+def adam_kernel(
+    where_ref, weight_ref, gradient_ref, first_ref, second_ref, far_ref, w_ref, m_ref, v_ref
+):
+    moved = where_ref[1] == 1
+    for block in range(far_ref.shape[1]):
+        columns = pl.ds(block * LANES, LANES)
+        first = jnp.where(moved, far_ref[0, block].astype(jnp.float32), first_ref[0, :, columns])
+        second = jnp.where(moved, far_ref[1, block].astype(jnp.float32), second_ref[0, :, columns])
+        w_ref[0, :, columns], m_ref[0, :, columns], v_ref[0, :, columns] = adam_update(
+            weight_ref[:, columns], first, second, gradient_ref[:, columns].astype(jnp.float32)
+        )
+
+
+def adam_step(row_block, moved, full_weights, gradient, first, second, far):
+    _, rows, width = first.shape
+    blocks = width // LANES
+    step = STEP if blocks % STEP == 0 else 1
+    state = pl.BlockSpec((1, rows, step * LANES), lambda i, where: (0, 0, i))
+    grid_spec = pltpu.PrefetchScalarGridSpec(
+        num_scalar_prefetch=1,
+        grid=(blocks // step,),
+        in_specs=[
+            pl.BlockSpec((rows, step * LANES), lambda i, where: (where[0], i)),
+            pl.BlockSpec((rows, step * LANES), lambda i, where: (0, i)),
+            state,
+            state,
+            pl.BlockSpec((2, step, rows, LANES), lambda i, where: (0, i, 0, 0)),
+        ],
+        out_specs=[state, state, state],
+    )
+    return pl.pallas_call(
+        adam_kernel,
+        grid_spec=grid_spec,
+        out_shape=[
+            jax.ShapeDtypeStruct(first.shape, jnp.bfloat16),
+            jax.ShapeDtypeStruct(first.shape, jnp.float32),
+            jax.ShapeDtypeStruct(first.shape, jnp.float32),
+        ],
+    )(jnp.stack([row_block, moved]), full_weights, gradient, first, second, far)
 
 
 def table_lookup(lookup_table, positions):
@@ -38,9 +105,36 @@
     slots = 2 * capacity
     flip_mine = table_lookup(swap_flags, my_place)
 
-    across = [(0, 1), (1, 0)]
-    first_far = lax.ppermute(moment1.astype(jnp.bfloat16), "zh", across)
-    second_far = lax.ppermute(moment2.astype(jnp.bfloat16), "zh", across)
+    plane_flags = swap_flags[:plane]
+    order = jnp.cumsum(plane_flags) - 1
+    trading = order[-1] + 1
+    lines = jnp.arange(plane, dtype=jnp.int32)
+    taken = (order[None, :] == lines[:, None]) & (plane_flags[None, :] == 1)
+    nth = jnp.sum(jnp.where(taken, lines[None, :], 0), axis=1)
+    order = jnp.maximum(order, 0)
+    sizes = sorted({max(1, plane * part // 32) for part in (8, 12, 14, 16, 18, 20, 22, 24, 28, 32)})
+    chosen_size = sum((trading > size).astype(jnp.int32) for size in sizes[:-1])
+
+    def crossing(size):
+        def branch(blocks):
+            packed = jnp.take(blocks, nth[:size], axis=0, mode="clip")
+            packed = lax.ppermute(packed, "zh", [(0, 1), (1, 0)])
+            return jnp.take(packed, order, axis=0, mode="clip")
+
+        return branch
+
+    def cross(blocks):
+        return lax.switch(chosen_size, [crossing(size) for size in sizes], blocks)
+
+    moment_blocks = pack_moments(moment1, moment2)
+    spread_blocks = lax.all_to_all(
+        moment_blocks.reshape(plane, -1, rows_dp, LANES), "p", split_axis=0, concat_axis=0, tiled=True
+    )
+    mine = spread_blocks.shape[1]
+    spread_blocks = spread_blocks.reshape(plane, mine * rows_dp, LANES)
+    cut = mine * rows_dp // 2
+    early_far = cross(spread_blocks[:, :cut])
+    hidden, upstream, _ = lax.optimization_barrier((hidden, upstream, early_far))
     full_weights = lax.all_gather(weights[0], ("zh", "dp"), axis=0, tiled=True)
 
     target = table_lookup(placement, route_ids.reshape(-1))
@@ -78,7 +172,8 @@
     ).astype(jnp.bfloat16)
     gradient = lax.psum_scatter(
         partial, ("zh", "dp"), scatter_dimension=0, tiled=True
-    ).astype(jnp.float32)
+    )
+    full_weights, _ = lax.optimization_barrier((full_weights, partial))
 
     terms = jnp.dot(spread, full_weights, preferred_element_type=jnp.float32).astype(jnp.bfloat16)
     back_terms = lax.all_to_all(
@@ -101,14 +196,16 @@
         tokens_here, chosen, hidden_width
     )
 
+    late_blocks, _, _ = lax.optimization_barrier((spread_blocks[:, cut:], terms, row_grads))
+    late_far = cross(late_blocks)
+    far = jnp.concatenate([early_far, late_far], axis=1).reshape(plane, mine, rows_dp, LANES)
+    far = lax.all_to_all(far, "p", split_axis=0, concat_axis=0, tiled=True)
     old_half = my_half ^ flip_mine
-    weight_here = lax.dynamic_slice_in_dim(
-        full_weights, old_half * hidden_width + my_dp * rows_dp, rows_dp, 0
-    )
-    first_here = jnp.where(flip_mine == 1, first_far[0].astype(jnp.float32), moment1[0])
-    second_here = jnp.where(flip_mine == 1, second_far[0].astype(jnp.float32), moment2[0])
-    new_w, new_first, new_second = adam_update(weight_here, first_here, second_here, gradient)
-    return (layer_out, hidden_grads, new_w[None], new_first[None], new_second[None])
+    row_block = old_half * (hidden_width // rows_dp) + my_dp
+    new_w, new_first, new_second = adam_step(
+        row_block, flip_mine, full_weights, gradient, moment1, moment2, far.reshape(moment_blocks.shape)
+    )
+    return (layer_out, hidden_grads, new_w, new_first, new_second)
 
 
 def solution(mesh):

time: 273 us -> 244 us (0.89)
  waiting for transfers between devices: 176 us -> 120 us
  starting transfers between devices: 44.1 us -> 65.4 us
  Pallas kernels: 0 us -> 8.32 us
  other arithmetic: 14.6 us -> 10 us
    all_gather x1, waiting for transfers between devices: 55.6 us -> 7.37 us  [shards(): full_weights = lax.all_gather(weights[0], ('zh', 'dp'), axis=0, tiled=True)]
    ppermute x2, waiting for transfers between devices: 75.1 us -> 55.3 us  [branch(): packed = lax.ppermute(packed, 'zh', [(0, 1), (1, 0)])]
    all_to_all x0 -> x2, starting transfers between devices: none -> 17.1 us  [the longest x1 9.45 us: shards(): lax.all_to_all(moment_blocks.reshape(plane, -1, rows_dp, LANES), 'p', spl...]
    all_to_all x0 -> x2, waiting for transfers between devices: none -> 16.1 us  [the longest x1 9.62 us: shards(): lax.all_to_all(moment_blocks.reshape(plane, -1, rows_dp, LANES), 'p', spl...]
    reduce_scatter x1, waiting for transfers between devices: 31.6 us -> 20.8 us  [shards(): lax.psum_scatter(partial, ('zh', 'dp'), scatter_dimension=0, tiled=True)]
    pallas_call x0 -> x2, Pallas kernels: none -> 8.32 us  [the longest x1 4.82 us: adam_step(): pl.pallas_call(adam_kernel, grid_spec=grid_spec, out_shape=[jax.ShapeDtyp...]
    ppermute x2, starting transfers between devices: 14.5 us -> 22.1 us  [branch(): packed = lax.ppermute(packed, 'zh', [(0, 1), (1, 0)])]
    all_to_all x1, waiting for transfers between devices: 0.01 us -> 5.42 us  [shards(): lax.all_to_all(send_hidden, 'p', split_axis=0, concat_axis=0, tiled=True)]
  transfers between devices with their start and end apart: 8 -> 10, of which waited for: 6 -> 9; matrix products, arithmetic and copies ran while one was open for 10% -> 13% of each run, Pallas kernels for 0% -> 1%
where the time goes in v2:
time: 244 us; the launch traced here: 242 us
  waiting for transfers between devices  120 us (49%)
  starting transfers between devices  65.4 us (27%)
  between operations  15.7 us (6%)
  matrix products  14.7 us (6%)
  other arithmetic  10 us (4%)
  Pallas kernels  8.32 us (3%)
  local copies, waits for them, and re-layouts  7.8 us (3%)
    ppermute x2, waiting for transfers between devices, branch(): packed = lax.ppermute(packed, 'zh', [(0, 1), (1, 0)])  55.3 us
    ppermute x2, starting transfers between devices, branch(): packed = lax.ppermute(packed, 'zh', [(0, 1), (1, 0)])  22.1 us
    reduce_scatter x1, waiting for transfers between devices, shards(): lax.psum_scatter(partial, ('zh', 'dp'), scatter_dimension=0, tiled=True)  20.8 us
    all_to_all x1, waiting for transfers between devices, shards(): lax.all_to_all(send_grads, 'p', split_axis=0, concat_axis=0, tiled=True)  12.3 us
    all_to_all x1, waiting for transfers between devices, shards(): lax.all_to_all(moment_blocks.reshape(plane, -1, rows_dp, LANES), 'p', spl...  9.62 us
    all_to_all x1, starting transfers between devices, shards(): lax.all_to_all(moment_blocks.reshape(plane, -1, rows_dp, LANES), 'p', spl...  9.45 us
    all_to_all x1, starting transfers between devices, shards(): far = lax.all_to_all(far, 'p', split_axis=0, concat_axis=0, tiled=True)  7.64 us
    all_to_all x1, starting transfers between devices, shards(): lax.all_to_all(row_grads.reshape(plane, slots, hidden_width), 'p', split_...  7.38 us
  transfers between devices with their start and end apart: 10, of which 9 were waited for; matrix products, arithmetic and copies ran while one was open for 13% of the time, Pallas kernels for 1%

profile of v2, /device:TPU:6, one launch (start us, length us, event | category | flops | bytes accessed | tf_op | source)
XLA Modules:
  0.0 242.5 jit_solution(8704940964583362287)
XLA Ops:
  7.9 3.5 %shard_map.128 = bf16[2,16,96,128]{3,2,1,0:T(8,128)(2,1)} custom-call(f32[1,96,2048]{2,1,0:T(8,128)} %first_ref.3, f32[1,96,2048]{2,1,0:T(8,128)} %second_ref.3), custom_call_target="tpu_custom_call" | custom-call | tf_op jit(solution)/shard_map/pallas_call | solution.py:38
  11.4 9.4 %all-to-all-start = ((bf16[32,1,96,128]{3,2,1,0:T(8,128)(2,1)}), bf16[32,1,96,128]{3,2,1,0:T(8,128)(2,1)S(1)}, u32[]{:S(2)}, u32[]{:S(2)}) async-start(bf16[32,1,96,128]{3,2,1,0:T(8,128)(2,1)} %bitcast.92), calls=%async_computation | async-start | bytes 1572864 | tf_op jit(solution)/shard_map/all_to_all | solution.py:130
  23.4 9.6 %all-to-all-done = bf16[32,1,96,128]{3,2,1,0:T(8,128)(2,1)S(1)} async-done(((bf16[32,1,96,128]{3,2,1,0:T(8,128)(2,1)}), bf16[32,1,96,128]{3,2,1,0:T(8,128)(2,1)S(1)}, u32[]{:S(2)}, u32[]{:S(2)}) %all-to-all-start) | async-done | bytes 786464 | tf_op jit(solution)/shard_map/all_to_all | solution.py:130
  33.1 40.1 %conditional.2 = (bf16[32,48,128]{2,1,0:T(8,128)(2,1)S(1)}) conditional(s32[]{:T(128)} %bitcast.4, (s32[32]{0:T(128)S(1)}, bf16[32,48,128]{2,1,0:T(8,128)(2,1)S(1)}, s32[32]{0:T(128)S(1)}) %tuple.71, (s32[32]{0:T(128)S(1)}, bf16[32,48,128]{2,1,0:T(8,128)(2,1)S(1)}, s32[32]{0:T(128)S(1)}) %tuple.71, (s32[32]{0:T(128)S(1)}, ...), branch_computations={%region_5.6_spmd, %region_6.7_spmd, %region_7.8_spmd, %region_8.9_... | conditional | flops 2048 | bytes 3154480 | solution.py:127
  33.7 13.8 %collective-permute-start.5 = (bf16[20,48,128]{2,1,0:T(8,128)(2,1)S(1)}, bf16[20,48,128]{2,1,0:T(8,128)(2,1)S(1)}, u32[]{:S(2)}, u32[]{:S(2)}) collective-permute-start(bf16[20,48,128]{2,1,0:T(8,128)(2,1)S(1)} %gather_fusion.10), channel_id=1, source_target_pairs={{0,32},{32,0},{1,33},{33,1},{2,34},{34,2},{3,35},{35,3},{4,36},{36... | collective-permute-start | bytes 737288 | tf_op jit(solution)/shard_map/cond/branch_5_fun/ppermute | solution.py:121
  47.5 25.0 %collective-permute-done.5 = bf16[20,48,128]{2,1,0:T(8,128)(2,1)S(1)} collective-permute-done((bf16[20,48,128]{2,1,0:T(8,128)(2,1)S(1)}, bf16[20,48,128]{2,1,0:T(8,128)(2,1)S(1)}, u32[]{:S(2)}, u32[]{:S(2)}) %collective-permute-start.5) | collective-permute-done | bytes 245792 | tf_op jit(solution)/shard_map/cond/branch_5_fun/ppermute | solution.py:121
  73.2 1.9 scatter_custom_fusion
  75.1 6.5 %all-to-all-start.1 = ((bf16[32,8,768]{2,1,0:T(8,128)(2,1)}), bf16[32,8,768]{2,1,0:T(8,128)(2,1)S(1)}, u32[]{:S(2)}, u32[]{:S(2)}) async-start(bf16[32,8,768]{2,1,0:T(8,128)(2,1)} %bitcast.9), calls=%async_computation.1 | async-start | bytes 786432 | tf_op jit(solution)/shard_map/all_to_all | solution.py:149
  81.7 2.5 %scatter_custom_fusion.1 = bf16[256,2048]{1,0:T(8,128)(2,1)} fusion(s32[128]{0:T(128)S(1)} %fusion.25, f32[16,2048]{1,0:T(8,128)S(1)} %convert_element_type.111, f32[128]{0:T(128)S(1)} %mul.64, bf16[]{:T(256)} %constant.120.clone.1), kind=kCustom, calls=%fused_computation.100 | custom fusion | flops 524288 | bytes 1180162 | tf_op jit(solution)/shard_map/scatter | solution.py:154
  84.2 5.4 %all-to-all-done.1 = bf16[32,8,768]{2,1,0:T(8,128)(2,1)S(1)} async-done(((bf16[32,8,768]{2,1,0:T(8,128)(2,1)}), bf16[32,8,768]{2,1,0:T(8,128)(2,1)S(1)}, u32[]{:S(2)}, u32[]{:S(2)}) %all-to-all-start.1) | async-done | bytes 393248 | tf_op jit(solution)/shard_map/all_to_all | solution.py:149
  89.7 6.1 %all-to-all-start.2 = ((bf16[32,8,2048]{2,1,0:T(8,128)(2,1)}), bf16[32,8,2048]{2,1,0:T(8,128)(2,1)S(1)}, u32[]{:S(2)}, u32[]{:S(2)}) async-start(bf16[32,8,2048]{2,1,0:T(8,128)(2,1)} %bitcast.13), calls=%async_computation.2 | async-start | bytes 2097152 | tf_op jit(solution)/shard_map/all_to_all | solution.py:156
  97.1 1.1 bitcast_select_fusion.3
  98.2 12.3 %all-to-all-done.2 = bf16[32,8,2048]{2,1,0:T(8,128)(2,1)S(1)} async-done(((bf16[32,8,2048]{2,1,0:T(8,128)(2,1)}), bf16[32,8,2048]{2,1,0:T(8,128)(2,1)S(1)}, u32[]{:S(2)}, u32[]{:S(2)}) %all-to-all-start.2) | async-done | bytes 1048608 | tf_op jit(solution)/shard_map/all_to_all | solution.py:156
  110.5 4.4 %convolution_convert_fusion = bf16[1536,2048]{1,0:T(8,128)(2,1)} fusion(bf16[32,8,2048]{2,1,0:T(8,128)(2,1)S(1)} %all-to-all-done.2, bf16[256,768]{1,0:T(8,128)(2,1)S(1)} %get-tuple-element.226, bf16[256,768]{1,0:T(8,128)(2,1)S(1)} %get-tuple-element.225), kind=kOutput, calls=%fused_computation.84 | convolution fusion | flops 1615331328 | bytes 8126464 | tf_op jit(solution)/shard_map/dot_general | solution.py:170
  115.0 7.4 %all-gather.3.cloned.1.call-done = bf16[1,1536,2048]{2,1,0:T(8,128)(2,1)} async-done(((bf16[1,96,2048]{2,1,0:T(8,128)(2,1)}), bf16[1,1536,2048]{2,1,0:T(8,128)(2,1)}) %all-gather.3.cloned.1.call-update) | async-done | bytes 6291472 | tf_op jit(solution)/shard_map/all_gather | solution.py:138
  122.3 4.7 %convolution_convert_fusion.1 = bf16[256,1536]{1,0:T(8,128)(2,1)S(1)} fusion(bf16[1536,2048]{1,0:T(8,128)(2,1)} %bitcast.87, bf16[32,8,2048]{2,1,0:T(8,128)(2,1)S(1)} %all-to-all-done.2), kind=kOutput, calls=%fused_computation.85 | convolution fusion | flops 1611005952 | bytes 8126464 | tf_op jit(solution)/shard_map/dot_general | solution.py:182
  127.9 7.4 %all-to-all-start.4 = ((bf16[32,8,768]{2,1,0:T(8,128)(2,1)}), bf16[32,8,768]{2,1,0:T(8,128)(2,1)S(1)}, u32[]{:S(2)}, u32[]{:S(2)}) async-start(bf16[32,8,768]{2,1,0:T(8,128)(2,1)} %fusion.32), calls=%async_computation.4 | async-start | bytes 786432 | tf_op jit(solution)/shard_map/all_to_all | solution.py:186
  135.3 5.6 %convolution_convert_fusion.2 = bf16[256,2048]{1,0:T(8,128)(2,1)} fusion(bf16[1536,2048]{1,0:T(8,128)(2,1)} %bitcast.88, bf16[256,768]{1,0:T(8,128)(2,1)S(1)} %copy-done.3, bf16[256,768]{1,0:T(8,128)(2,1)S(1)} %copy-done.2), kind=kOutput, calls=%fused_computation.86 | convolution fusion | flops 1612709888 | bytes 8126464 | tf_op jit(solution)/shard_map/dot_general | solution.py:178
  140.9 2.4 all-to-all-done.4
  143.3 6.1 %all-to-all-start.3 = ((bf16[32,8,2048]{2,1,0:T(8,128)(2,1)}), bf16[32,8,2048]{2,1,0:T(8,128)(2,1)S(1)}, u32[]{:S(2)}, u32[]{:S(2)}) async-start(bf16[32,8,2048]{2,1,0:T(8,128)(2,1)} %bitcast.15), calls=%async_computation.3 | async-start | bytes 2097152 | tf_op jit(solution)/shard_map/all_to_all | solution.py:179
  149.4 40.0 %conditional.3 = (bf16[32,48,128]{2,1,0:T(8,128)(2,1)S(1)}) conditional(s32[]{:T(128)} %bitcast.4, (s32[32]{0:T(128)S(1)}, bf16[32,48,128]{2,1,0:T(8,128)(2,1)S(1)}, s32[32]{0:T(128)S(1)}) %tuple.75, (s32[32]{0:T(128)S(1)}, bf16[32,48,128]{2,1,0:T(8,128)(2,1)S(1)}, s32[32]{0:T(128)S(1)}) %tuple.75, (s32[32]{0:T(128)S(1)}, ...), branch_computations={%region_20.21_spmd, %region_21.22_spmd, %region_22.23_spmd, %regio... | conditional | flops 2048 | bytes 3154480 | solution.py:127
  150.1 8.4 %collective-permute-start.15 = (bf16[20,48,128]{2,1,0:T(8,128)(2,1)S(1)}, bf16[20,48,128]{2,1,0:T(8,128)(2,1)S(1)}, u32[]{:S(2)}, u32[]{:S(2)}) collective-permute-start(bf16[20,48,128]{2,1,0:T(8,128)(2,1)S(1)} %gather_fusion.30), channel_id=1, source_target_pairs={{0,32},{32,0},{1,33},{33,1},{2,34},{34,2},{3,35},{35,3},{4,36},{36... | collective-permute-start | bytes 737288 | tf_op jit(solution)/shard_map/cond/branch_5_fun/ppermute | solution.py:121
  158.5 30.3 %collective-permute-done.15 = bf16[20,48,128]{2,1,0:T(8,128)(2,1)S(1)} collective-permute-done((bf16[20,48,128]{2,1,0:T(8,128)(2,1)S(1)}, bf16[20,48,128]{2,1,0:T(8,128)(2,1)S(1)}, u32[]{:S(2)}, u32[]{:S(2)}) %collective-permute-start.15) | collective-permute-done | bytes 245792 | tf_op jit(solution)/shard_map/cond/branch_5_fun/ppermute | solution.py:121
  189.4 0.9 maximum_bitcast_fusion
  190.3 7.6 %all-to-all-start.5 = ((bf16[32,1,96,128]{3,2,1,0:T(8,128)(2,1)}), bf16[32,1,96,128]{3,2,1,0:T(8,128)(2,1)S(1)}, u32[]{:S(2)}, u32[]{:S(2)}) async-start(bf16[32,1,96,128]{3,2,1,0:T(8,128)(2,1)} %maximum_bitcast_fusion), calls=%async_computation.6 | async-start | bytes 1572864 | tf_op jit(solution)/shard_map/all_to_all | solution.py:202
  198.6 1.3 pad_add_fusion.where_ref
  199.9 1.5 gather_fusion.41
  201.5 0.9 gather_fusion.40
  202.4 1.1 fusion
  203.5 6.5 %all-to-all-done.5 = bf16[32,1,96,128]{3,2,1,0:T(8,128)(2,1)S(1)} async-done(((bf16[32,1,96,128]{3,2,1,0:T(8,128)(2,1)}), bf16[32,1,96,128]{3,2,1,0:T(8,128)(2,1)S(1)}, u32[]{:S(2)}, u32[]{:S(2)}) %all-to-all-start.5) | async-done | bytes 786464 | tf_op jit(solution)/shard_map/all_to_all | solution.py:202
  210.0 20.8 %reduce-scatter.2.cloned.1.call-done.gradient_ref = bf16[96,2048]{1,0:T(8,128)(2,1)} async-done(((bf16[1536,2048]{1,0:T(8,128)(2,1)}), bf16[96,2048]{1,0:T(8,128)(2,1)}) %reduce-scatter.2.cloned.1.call-update) | async-done | bytes 393232 | tf_op jit(solution)/shard_map/reduce_scatter | solution.py:173
  230.8 4.8 %shard_map.129 = (bf16[1,96,2048]{2,1,0:T(8,128)(2,1)}, f32[1,96,2048]{2,1,0:T(8,128)}, f32[1,96,2048]{2,1,0:T(8,128)}) custom-call(s32[2]{0:T(128)} %pad_add_fusion.where_ref, bf16[1536,2048]{1,0:T(8,128)(2,1)} %bitcast.89, bf16[96,2048]{1,0:T(8,128)(2,1)} %reduce-scatter.2.cloned.1.call-done.gradient_ref, f32[1,96,2048]{2,1,0:T(8,128)} %first_ref.3, ...), custom_call_target="tpu_custom_call" | custom-call | tf_op jit(solution)/shard_map/pallas_call | solution.py:77
  (56 shorter events, 7.4 us)
Async XLA Ops:
  7.2 66.0 %copy-start = (bf16[16,8,768]{2,1,0:T(8,128)(2,1)S(1)}, bf16[16,8,768]{2,1,0:T(8,128)(2,1)}, u32[]{:S(2)}) copy-start(bf16[16,8,768]{2,1,0:T(8,128)(2,1)} %param.31) | copy-start | bytes 589828
  7.2 13.7 %copy-start.5 = (s32[16,8]{0,1:T(8,128)S(1)}, s32[16,8]{0,1:T(8,128)}, u32[]{:S(2)}) copy-start(s32[16,8]{0,1:T(8,128)} %param.29) | copy-start | bytes 1540
  7.2 13.9 %copy-start.8 = (s32[64]{0:T(128)S(1)}, s32[64]{0:T(128)}, u32[]{:S(2)}) copy-start(s32[64]{0:T(128)} %param.34) | copy-start | bytes 772
  7.2 115.1 %all-gather.3.cloned.1.call-start = ((), (), s32[]{:S(2)}) async-start(), calls=%async_computation.8 | async-start | bytes 6684672 | tf_op jit(solution)/shard_map/all_gather | solution.py:138
  7.9 13.3 %copy-start.7 = (s32[64]{0:T(128)S(1)}, s32[64]{0:T(128)}, u32[]{:S(2)}) copy-start(s32[64]{0:T(128)} %param.33) | copy-start | bytes 772
  11.4 21.5 %all-to-all-start = ((bf16[32,1,96,128]{3,2,1,0:T(8,128)(2,1)}), bf16[32,1,96,128]{3,2,1,0:T(8,128)(2,1)S(1)}, u32[]{:S(2)}, u32[]{:S(2)}) async-start(bf16[32,1,96,128]{3,2,1,0:T(8,128)(2,1)} %bitcast.92), calls=%async_computation | async-start | bytes 1572864 | tf_op jit(solution)/shard_map/all_to_all | solution.py:130
  33.0 48.5 %copy-start.6 = (f32[16,8]{0,1:T(8,128)S(1)}, f32[16,8]{0,1:T(8,128)}, u32[]{:S(2)}) copy-start(f32[16,8]{0,1:T(8,128)} %param.30) | copy-start | bytes 1540
  33.0 48.7 %copy-start.4 = (bf16[16,2048]{1,0:T(8,128)(2,1)S(1)}, bf16[16,2048]{1,0:T(8,128)(2,1)}, u32[]{:S(2)}) copy-start(bf16[16,2048]{1,0:T(8,128)(2,1)} %param.32) | copy-start | bytes 196612
  33.7 38.8 %collective-permute-start.5 = (bf16[20,48,128]{2,1,0:T(8,128)(2,1)S(1)}, bf16[20,48,128]{2,1,0:T(8,128)(2,1)S(1)}, u32[]{:S(2)}, u32[]{:S(2)}) collective-permute-start(bf16[20,48,128]{2,1,0:T(8,128)(2,1)S(1)} %gather_fusion.10), channel_id=1, source_target_pairs={{0,32},{32,0},{1,33},{33,1},{2,34},{34,2},{3,35},{35,3},{4,36},{36... | collective-permute-start | bytes 737288 | tf_op jit(solution)/shard_map/cond/branch_5_fun/ppermute | solution.py:121
  75.1 14.6 %all-to-all-start.1 = ((bf16[32,8,768]{2,1,0:T(8,128)(2,1)}), bf16[32,8,768]{2,1,0:T(8,128)(2,1)S(1)}, u32[]{:S(2)}, u32[]{:S(2)}) async-start(bf16[32,8,768]{2,1,0:T(8,128)(2,1)} %bitcast.9), calls=%async_computation.1 | async-start | bytes 786432 | tf_op jit(solution)/shard_map/all_to_all | solution.py:149
  89.7 20.8 %all-to-all-start.2 = ((bf16[32,8,2048]{2,1,0:T(8,128)(2,1)}), bf16[32,8,2048]{2,1,0:T(8,128)(2,1)S(1)}, u32[]{:S(2)}, u32[]{:S(2)}) async-start(bf16[32,8,2048]{2,1,0:T(8,128)(2,1)} %bitcast.13), calls=%async_computation.2 | async-start | bytes 2097152 | tf_op jit(solution)/shard_map/all_to_all | solution.py:156
  95.8 135.0 %reduce-scatter.2.cloned.1.call-start = ((), (), s32[]{:S(2)}) async-start(), calls=%async_computation.7 | async-start | bytes 6684672 | tf_op jit(solution)/shard_map/reduce_scatter | solution.py:173
  122.3 12.9 %copy-start.2 = (bf16[256,768]{1,0:T(8,128)(2,1)S(1)}, bf16[256,768]{1,0:T(8,128)(2,1)}, u32[]{:S(2)}) copy-start(bf16[256,768]{1,0:T(8,128)(2,1)} %get-tuple-element.223) | copy-start | bytes 1179652
  122.3 12.9 %copy-start.3 = (bf16[256,768]{1,0:T(8,128)(2,1)S(1)}, bf16[256,768]{1,0:T(8,128)(2,1)}, u32[]{:S(2)}) copy-start(bf16[256,768]{1,0:T(8,128)(2,1)} %get-tuple-element.224) | copy-start | bytes 1179652
  127.9 15.4 %all-to-all-start.4 = ((bf16[32,8,768]{2,1,0:T(8,128)(2,1)}), bf16[32,8,768]{2,1,0:T(8,128)(2,1)S(1)}, u32[]{:S(2)}, u32[]{:S(2)}) async-start(bf16[32,8,768]{2,1,0:T(8,128)(2,1)} %fusion.32), calls=%async_computation.4 | async-start | bytes 786432 | tf_op jit(solution)/shard_map/all_to_all | solution.py:186
  143.3 47.0 %all-to-all-start.3 = ((bf16[32,8,2048]{2,1,0:T(8,128)(2,1)}), bf16[32,8,2048]{2,1,0:T(8,128)(2,1)S(1)}, u32[]{:S(2)}, u32[]{:S(2)}) async-start(bf16[32,8,2048]{2,1,0:T(8,128)(2,1)} %bitcast.15), calls=%async_computation.3 | async-start | bytes 2097152 | tf_op jit(solution)/shard_map/all_to_all | solution.py:179
  150.1 38.7 %collective-permute-start.15 = (bf16[20,48,128]{2,1,0:T(8,128)(2,1)S(1)}, bf16[20,48,128]{2,1,0:T(8,128)(2,1)S(1)}, u32[]{:S(2)}, u32[]{:S(2)}) collective-permute-start(bf16[20,48,128]{2,1,0:T(8,128)(2,1)S(1)} %gather_fusion.30), channel_id=1, source_target_pairs={{0,32},{32,0},{1,33},{33,1},{2,34},{34,2},{3,35},{35,3},{4,36},{36... | collective-permute-start | bytes 737288 | tf_op jit(solution)/shard_map/cond/branch_5_fun/ppermute | solution.py:121
  190.3 19.6 %all-to-all-start.5 = ((bf16[32,1,96,128]{3,2,1,0:T(8,128)(2,1)}), bf16[32,1,96,128]{3,2,1,0:T(8,128)(2,1)S(1)}, u32[]{:S(2)}, u32[]{:S(2)}) async-start(bf16[32,1,96,128]{3,2,1,0:T(8,128)(2,1)} %maximum_bitcast_fusion), calls=%async_computation.6 | async-start | bytes 1572864 | tf_op jit(solution)/shard_map/all_to_all | solution.py:202
  210.0 20.8 %copy-start.1 = (bf16[32,1,96,128]{3,2,1,0:T(8,128)(2,1)}, bf16[32,1,96,128]{3,2,1,0:T(8,128)(2,1)S(1)}, u32[]{:S(2)}) copy-start(bf16[32,1,96,128]{3,2,1,0:T(8,128)(2,1)S(1)} %all-to-all-done.5) | copy-start | bytes 2359300
Sparse Core Ops, SparseCore 0:
  10.1 112.1 all-gather.2
  125.2 105.5 reduce-scatter.1

commit v3 on v2

--- a/solution.py
+++ b/solution.py
@@ -14,12 +14,14 @@
 
 
 LANES, STEP = 128, 4
-
-
-def adam_update(weight, first, second, gradient):
-    new_first = decay_one * first + (1.0 - decay_one) * gradient
-    new_second = decay_two * second + (1.0 - decay_two) * gradient * gradient
-    step_size = learn_rate * (new_first / bias_one) / (jnp.sqrt(new_second / bias_two) + epsilon)
+PARTS = (4, 8, 10, 12, 13, 14, 15, 16, 17, 18, 19, 20, 21, 22, 24, 26, 28, 32)
+
+
+def adam_update(weight, decayed_first, decayed_second, gradient):
+    new_first = decayed_first + (1.0 - decay_one) * gradient
+    new_second = decayed_second + (1.0 - decay_two) * gradient * gradient
+    spread = jnp.sqrt(new_second * (1.0 / bias_two)) + epsilon
+    step_size = new_first * (learn_rate / bias_one) / spread
     return ((weight.astype(jnp.float32) - step_size).astype(jnp.bfloat16), new_first, new_second)
 
 
@@ -44,20 +46,18 @@
     )(first, second)
 
 
-def adam_kernel(
-    where_ref, weight_ref, gradient_ref, first_ref, second_ref, far_ref, w_ref, m_ref, v_ref
-):
+def home_kernel(where_ref, weight_ref, first_ref, second_ref, far_ref, w_ref, m_ref, v_ref):
     moved = where_ref[1] == 1
+    w_ref[0] = weight_ref[...]
     for block in range(far_ref.shape[1]):
         columns = pl.ds(block * LANES, LANES)
         first = jnp.where(moved, far_ref[0, block].astype(jnp.float32), first_ref[0, :, columns])
         second = jnp.where(moved, far_ref[1, block].astype(jnp.float32), second_ref[0, :, columns])
-        w_ref[0, :, columns], m_ref[0, :, columns], v_ref[0, :, columns] = adam_update(
-            weight_ref[:, columns], first, second, gradient_ref[:, columns].astype(jnp.float32)
-        )
-
-
-def adam_step(row_block, moved, full_weights, gradient, first, second, far):
+        m_ref[0, :, columns] = decay_one * first
+        v_ref[0, :, columns] = decay_two * second
+
+
+def state_at_home(row_block, moved, full_weights, first, second, far):
     _, rows, width = first.shape
     blocks = width // LANES
     step = STEP if blocks % STEP == 0 else 1
@@ -67,7 +67,6 @@
         grid=(blocks // step,),
         in_specs=[
             pl.BlockSpec((rows, step * LANES), lambda i, where: (where[0], i)),
-            pl.BlockSpec((rows, step * LANES), lambda i, where: (0, i)),
             state,
             state,
             pl.BlockSpec((2, step, rows, LANES), lambda i, where: (0, i, 0, 0)),
@@ -75,14 +74,14 @@
         out_specs=[state, state, state],
     )
     return pl.pallas_call(
-        adam_kernel,
+        home_kernel,
         grid_spec=grid_spec,
         out_shape=[
             jax.ShapeDtypeStruct(first.shape, jnp.bfloat16),
             jax.ShapeDtypeStruct(first.shape, jnp.float32),
             jax.ShapeDtypeStruct(first.shape, jnp.float32),
         ],
-    )(jnp.stack([row_block, moved]), full_weights, gradient, first, second, far)
+    )(jnp.stack([row_block, moved]), full_weights, first, second, far)
 
 
 def table_lookup(lookup_table, positions):
@@ -112,7 +111,7 @@
     taken = (order[None, :] == lines[:, None]) & (plane_flags[None, :] == 1)
     nth = jnp.sum(jnp.where(taken, lines[None, :], 0), axis=1)
     order = jnp.maximum(order, 0)
-    sizes = sorted({max(1, plane * part // 32) for part in (8, 12, 14, 16, 18, 20, 22, 24, 28, 32)})
+    sizes = sorted({max(1, plane * part // 32) for part in PARTS})
     chosen_size = sum((trading > size).astype(jnp.int32) for size in sizes[:-1])
 
     def crossing(size):
@@ -202,8 +201,11 @@
     far = lax.all_to_all(far, "p", split_axis=0, concat_axis=0, tiled=True)
     old_half = my_half ^ flip_mine
     row_block = old_half * (hidden_width // rows_dp) + my_dp
-    new_w, new_first, new_second = adam_step(
-        row_block, flip_mine, full_weights, gradient, moment1, moment2, far.reshape(moment_blocks.shape)
+    weight_here, first_here, second_here = state_at_home(
+        row_block, flip_mine, full_weights, moment1, moment2, far.reshape(moment_blocks.shape)
+    )
+    new_w, new_first, new_second = adam_update(
+        weight_here, first_here, second_here, gradient[None].astype(jnp.float32)
     )
     return (layer_out, hidden_grads, new_w, new_first, new_second)
 

time: 244 us -> 250 us (1.025)
  blocking collectives: 0 us -> 19.2 us
  starting transfers between devices: 65.4 us -> 58.2 us
  waiting for transfers between devices: 120 us -> 113 us
    all_to_all x0 -> x1, blocking collectives: none -> 19.2 us  [shards(): far = lax.all_to_all(far, 'p', split_axis=0, concat_axis=0, tiled=True)]
    reduce_scatter x1, waiting for transfers between devices: 20.8 us -> 6.13 us  [shards(): lax.psum_scatter(partial, ('zh', 'dp'), scatter_dimension=0, tiled=True)]
    ppermute x2, waiting for transfers between devices: 55.3 us -> 66.3 us  [branch(): packed = lax.ppermute(packed, 'zh', [(0, 1), (1, 0)])]
    all_to_all x1 -> x0, starting transfers between devices: 7.64 us -> none  [shards(): far = lax.all_to_all(far, 'p', split_axis=0, concat_axis=0, tiled=True)]
    all_to_all x1, waiting for transfers between devices: 0.01 us -> 6.55 us  [shards(): lax.all_to_all(terms.reshape(plane, slots, width), 'p', split_axis=0, con...]
    all_to_all x1 -> x0, waiting for transfers between devices: 6.46 us -> none  [shards(): far = lax.all_to_all(far, 'p', split_axis=0, concat_axis=0, tiled=True)]
    convert_element_type x0 -> x1, other arithmetic: none -> 2.84 us  [adam_update(): (weight.astype(jnp.float32) - step_size).astype(jnp.bfloat16)]
  transfers between devices with their start and end apart: 10 -> 9, of which waited for: 9 -> 8; matrix products, arithmetic and copies ran while one was open for 13% -> 13% of each run, Pallas kernels for 1% -> 3%
where the time goes in v3:
time: 250 us; the launch traced here: 249 us
  waiting for transfers between devices  113 us (45%)
  starting transfers between devices  58.2 us (23%)
  blocking collectives  19.2 us (8%)
  between operations  15.7 us (6%)
  matrix products  14.7 us (6%)
  other arithmetic  12 us (5%)
  Pallas kernels  8.15 us (3%)
  local copies, waits for them, and re-layouts  7.82 us (3%)
    ppermute x2, waiting for transfers between devices, branch(): packed = lax.ppermute(packed, 'zh', [(0, 1), (1, 0)])  66.3 us
    ppermute x2, starting transfers between devices, branch(): packed = lax.ppermute(packed, 'zh', [(0, 1), (1, 0)])  22.1 us
    all_to_all x1, blocking collectives, shards(): far = lax.all_to_all(far, 'p', split_axis=0, concat_axis=0, tiled=True)  19.2 us
    all_to_all x1, waiting for transfers between devices, shards(): lax.all_to_all(send_grads, 'p', split_axis=0, concat_axis=0, tiled=True)  12.1 us
    all_to_all x1, waiting for transfers between devices, shards(): lax.all_to_all(moment_blocks.reshape(plane, -1, rows_dp, LANES), 'p', spl...  9.57 us
    all_to_all x1, starting transfers between devices, shards(): lax.all_to_all(moment_blocks.reshape(plane, -1, rows_dp, LANES), 'p', spl...  9.45 us
    all_to_all x1, starting transfers between devices, shards(): lax.all_to_all(row_grads.reshape(plane, slots, hidden_width), 'p', split_...  7.38 us
    all_to_all x1, waiting for transfers between devices, shards(): lax.all_to_all(terms.reshape(plane, slots, width), 'p', split_axis=0, con...  6.55 us
  transfers between devices with their start and end apart: 9, of which 8 were waited for; matrix products, arithmetic and copies ran while one was open for 13% of the time, Pallas kernels for 3%

profile of v3, /device:TPU:6, one launch (start us, length us, event | category | flops | bytes accessed | tf_op | source)
XLA Modules:
  0.0 248.9 jit_solution(7490042152679238780)
XLA Ops:
  7.9 3.5 %shard_map.128 = bf16[2,16,96,128]{3,2,1,0:T(8,128)(2,1)} custom-call(f32[1,96,2048]{2,1,0:T(8,128)} %first_ref.3, f32[1,96,2048]{2,1,0:T(8,128)} %second_ref.3), custom_call_target="tpu_custom_call" | custom-call | tf_op jit(solution)/shard_map/pallas_call | solution.py:40
  11.4 9.4 %all-to-all-start = ((bf16[32,1,96,128]{3,2,1,0:T(8,128)(2,1)}), bf16[32,1,96,128]{3,2,1,0:T(8,128)(2,1)S(1)}, u32[]{:S(2)}, u32[]{:S(2)}) async-start(bf16[32,1,96,128]{3,2,1,0:T(8,128)(2,1)} %bitcast.123), calls=%async_computation | async-start | bytes 1572864 | tf_op jit(solution)/shard_map/all_to_all | solution.py:129
  23.4 9.6 %all-to-all-done = bf16[32,1,96,128]{3,2,1,0:T(8,128)(2,1)S(1)} async-done(((bf16[32,1,96,128]{3,2,1,0:T(8,128)(2,1)}), bf16[32,1,96,128]{3,2,1,0:T(8,128)(2,1)S(1)}, u32[]{:S(2)}, u32[]{:S(2)}) %all-to-all-start) | async-done | bytes 786464 | tf_op jit(solution)/shard_map/all_to_all | solution.py:129
  33.1 45.4 %conditional.2 = (bf16[32,48,128]{2,1,0:T(8,128)(2,1)S(1)}) conditional(s32[]{:T(128)} %clamp.4, (s32[32]{0:T(128)S(1)}, bf16[32,48,128]{2,1,0:T(8,128)(2,1)S(1)}, s32[32]{0:T(128)S(1)}) %tuple.119, (s32[32]{0:T(128)S(1)}, bf16[32,48,128]{2,1,0:T(8,128)(2,1)S(1)}, s32[32]{0:T(128)S(1)}) %tuple.119, (s32[32]{0:T(128)S(1)}, ...), branch_computations={%region_5.6_spmd, %region_6.7_spmd, %region_7.8_spmd, %region_8.9_... | conditional | flops 2048 | bytes 3154480 | solution.py:126
  33.7 13.8 %collective-permute-start.14 = (bf16[24,48,128]{2,1,0:T(8,128)(2,1)S(1)}, bf16[24,48,128]{2,1,0:T(8,128)(2,1)S(1)}, u32[]{:S(2)}, u32[]{:S(2)}) collective-permute-start(bf16[24,48,128]{2,1,0:T(8,128)(2,1)S(1)} %gather_fusion.28), channel_id=1, source_target_pairs={{0,32},{32,0},{1,33},{33,1},{2,34},{34,2},{3,35},{35,3},{4,36},{36... | collective-permute-start | bytes 884744 | tf_op jit(solution)/shard_map/cond/branch_14_fun/ppermute | solution.py:120
  47.5 30.3 %collective-permute-done.14 = bf16[24,48,128]{2,1,0:T(8,128)(2,1)S(1)} collective-permute-done((bf16[24,48,128]{2,1,0:T(8,128)(2,1)S(1)}, bf16[24,48,128]{2,1,0:T(8,128)(2,1)S(1)}, u32[]{:S(2)}, u32[]{:S(2)}) %collective-permute-start.14) | collective-permute-done | bytes 294944 | tf_op jit(solution)/shard_map/cond/branch_14_fun/ppermute | solution.py:120
  78.4 1.9 scatter_custom_fusion
  80.3 6.5 %all-to-all-start.1 = ((bf16[32,8,768]{2,1,0:T(8,128)(2,1)}), bf16[32,8,768]{2,1,0:T(8,128)(2,1)S(1)}, u32[]{:S(2)}, u32[]{:S(2)}) async-start(bf16[32,8,768]{2,1,0:T(8,128)(2,1)} %bitcast.14), calls=%async_computation.1 | async-start | bytes 786432 | tf_op jit(solution)/shard_map/all_to_all | solution.py:148
  87.0 2.5 %scatter_custom_fusion.1 = bf16[256,2048]{1,0:T(8,128)(2,1)} fusion(s32[128]{0:T(128)S(1)} %fusion.29, f32[16,2048]{1,0:T(8,128)S(1)} %convert_element_type.193, f32[128]{0:T(128)S(1)} %mul.98, bf16[]{:T(256)} %constant.147.clone.1), kind=kCustom, calls=%fused_computation.171 | custom fusion | flops 524288 | bytes 1180162 | tf_op jit(solution)/shard_map/scatter | solution.py:153
  89.5 5.4 %all-to-all-done.1 = bf16[32,8,768]{2,1,0:T(8,128)(2,1)S(1)} async-done(((bf16[32,8,768]{2,1,0:T(8,128)(2,1)}), bf16[32,8,768]{2,1,0:T(8,128)(2,1)S(1)}, u32[]{:S(2)}, u32[]{:S(2)}) %all-to-all-start.1) | async-done | bytes 393248 | tf_op jit(solution)/shard_map/all_to_all | solution.py:148
  94.9 6.1 %all-to-all-start.2 = ((bf16[32,8,2048]{2,1,0:T(8,128)(2,1)}), bf16[32,8,2048]{2,1,0:T(8,128)(2,1)S(1)}, u32[]{:S(2)}, u32[]{:S(2)}) async-start(bf16[32,8,2048]{2,1,0:T(8,128)(2,1)} %bitcast.18), calls=%async_computation.2 | async-start | bytes 2097152 | tf_op jit(solution)/shard_map/all_to_all | solution.py:155
  102.6 1.1 bitcast_select_fusion.3
  103.7 12.1 %all-to-all-done.2 = bf16[32,8,2048]{2,1,0:T(8,128)(2,1)S(1)} async-done(((bf16[32,8,2048]{2,1,0:T(8,128)(2,1)}), bf16[32,8,2048]{2,1,0:T(8,128)(2,1)S(1)}, u32[]{:S(2)}, u32[]{:S(2)}) %all-to-all-start.2) | async-done | bytes 1048608 | tf_op jit(solution)/shard_map/all_to_all | solution.py:155
  115.8 4.5 %convolution_convert_fusion = bf16[1536,2048]{1,0:T(8,128)(2,1)} fusion(bf16[32,8,2048]{2,1,0:T(8,128)(2,1)S(1)} %all-to-all-done.2, bf16[256,768]{1,0:T(8,128)(2,1)S(1)} %get-tuple-element.389, bf16[256,768]{1,0:T(8,128)(2,1)S(1)} %get-tuple-element.388), kind=kOutput, calls=%fused_computation.148 | convolution fusion | flops 1615331328 | bytes 8126464 | tf_op jit(solution)/shard_map/dot_general | solution.py:169
  120.3 6.3 %all-gather.3.cloned.1.call-done = bf16[1,1536,2048]{2,1,0:T(8,128)(2,1)} async-done(((bf16[1,96,2048]{2,1,0:T(8,128)(2,1)}), bf16[1,1536,2048]{2,1,0:T(8,128)(2,1)}) %all-gather.3.cloned.1.call-update) | async-done | bytes 6291472 | tf_op jit(solution)/shard_map/all_gather | solution.py:137
  126.6 4.7 %convolution_convert_fusion.1 = bf16[256,1536]{1,0:T(8,128)(2,1)S(1)} fusion(bf16[1536,2048]{1,0:T(8,128)(2,1)} %bitcast.118, bf16[32,8,2048]{2,1,0:T(8,128)(2,1)S(1)} %all-to-all-done.2), kind=kOutput, calls=%fused_computation.149 | convolution fusion | flops 1611005952 | bytes 8126464 | tf_op jit(solution)/shard_map/dot_general | solution.py:181
  131.2 0.9 fusion.38
  132.1 7.4 %all-to-all-start.4 = ((bf16[32,8,768]{2,1,0:T(8,128)(2,1)}), bf16[32,8,768]{2,1,0:T(8,128)(2,1)S(1)}, u32[]{:S(2)}, u32[]{:S(2)}) async-start(bf16[32,8,768]{2,1,0:T(8,128)(2,1)} %fusion.38), calls=%async_computation.4 | async-start | bytes 786432 | tf_op jit(solution)/shard_map/all_to_all | solution.py:185
  139.5 5.5 %convolution_convert_fusion.2 = bf16[256,2048]{1,0:T(8,128)(2,1)} fusion(bf16[1536,2048]{1,0:T(8,128)(2,1)} %bitcast.119, bf16[256,768]{1,0:T(8,128)(2,1)S(1)} %copy-done.4, bf16[256,768]{1,0:T(8,128)(2,1)S(1)} %copy-done.3), kind=kOutput, calls=%fused_computation.150 | convolution fusion | flops 1612709888 | bytes 8126464 | tf_op jit(solution)/shard_map/dot_general | solution.py:177
  145.1 45.6 %conditional.3 = (bf16[32,48,128]{2,1,0:T(8,128)(2,1)S(1)}) conditional(s32[]{:T(128)} %clamp.4, (s32[32]{0:T(128)S(1)}, bf16[32,48,128]{2,1,0:T(8,128)(2,1)S(1)}, s32[32]{0:T(128)S(1)}) %tuple.123, (s32[32]{0:T(128)S(1)}, bf16[32,48,128]{2,1,0:T(8,128)(2,1)S(1)}, s32[32]{0:T(128)S(1)}) %tuple.123, (s32[32]{0:T(128)S(1)}, ...), branch_computations={%region_27.28_spmd, %region_28.29_spmd, %region_29.30_spmd, %regio... | conditional | flops 2048 | bytes 3154480 | solution.py:126
  145.7 8.4 %collective-permute-start.32 = (bf16[24,48,128]{2,1,0:T(8,128)(2,1)S(1)}, bf16[24,48,128]{2,1,0:T(8,128)(2,1)S(1)}, u32[]{:S(2)}, u32[]{:S(2)}) collective-permute-start(bf16[24,48,128]{2,1,0:T(8,128)(2,1)S(1)} %gather_fusion.64), channel_id=1, source_target_pairs={{0,32},{32,0},{1,33},{33,1},{2,34},{34,2},{3,35},{35,3},{4,36},{36... | collective-permute-start | bytes 884744 | tf_op jit(solution)/shard_map/cond/branch_14_fun/ppermute | solution.py:120
  154.0 36.0 %collective-permute-done.32 = bf16[24,48,128]{2,1,0:T(8,128)(2,1)S(1)} collective-permute-done((bf16[24,48,128]{2,1,0:T(8,128)(2,1)S(1)}, bf16[24,48,128]{2,1,0:T(8,128)(2,1)S(1)}, u32[]{:S(2)}, u32[]{:S(2)}) %collective-permute-start.32) | collective-permute-done | bytes 294944 | tf_op jit(solution)/shard_map/cond/branch_14_fun/ppermute | solution.py:120
  190.7 19.2 %all_to_all.30 = bf16[32,1,96,128]{3,2,1,0:T(8,128)(2,1)} all-to-all(bf16[32,1,96,128]{3,2,1,0:T(8,128)(2,1)S(1)} %maximum_bitcast_fusion), channel_id=1, replica_groups=mesh['dp'=8,'zh'=2,'p'=32] {'p'}, dimensions={0} | all-to-all | bytes 1572864 | tf_op jit(solution)/shard_map/all_to_all | solution.py:201
  210.0 6.4 %all-to-all-start.3 = ((bf16[32,8,2048]{2,1,0:T(8,128)(2,1)}), bf16[32,8,2048]{2,1,0:T(8,128)(2,1)S(1)}, u32[]{:S(2)}, u32[]{:S(2)}) async-start(bf16[32,8,2048]{2,1,0:T(8,128)(2,1)} %bitcast.20), calls=%async_computation.3 | async-start | bytes 2097152 | tf_op jit(solution)/shard_map/all_to_all | solution.py:178
  217.1 1.3 pad_add_fusion.where_ref
  218.4 1.5 gather_fusion.73
  219.9 4.7 %shard_map.129 = (bf16[1,96,2048]{2,1,0:T(8,128)(2,1)}, f32[1,96,2048]{2,1,0:T(8,128)}, f32[1,96,2048]{2,1,0:T(8,128)}) custom-call(s32[2]{0:T(128)} %pad_add_fusion.where_ref, bf16[1536,2048]{1,0:T(8,128)(2,1)} %bitcast.120, f32[1,96,2048]{2,1,0:T(8,128)} %first_ref.3, f32[1,96,2048]{2,1,0:T(8,128)} %second_ref.3, bf16[2,16,96,128]{3,2,1,0:T(8,128)(2,1)} %bitcast.121), custom_call_target="tpu_custom_call" | custom-call | tf_op jit(solution)/shard_map/pallas_call | solution.py:76
  224.6 6.5 %all-to-all-done.3 = bf16[32,8,2048]{2,1,0:T(8,128)(2,1)S(1)} async-done(((bf16[32,8,2048]{2,1,0:T(8,128)(2,1)}), bf16[32,8,2048]{2,1,0:T(8,128)(2,1)S(1)}, u32[]{:S(2)}, u32[]{:S(2)}) %all-to-all-start.3) | async-done | bytes 1048608 | tf_op jit(solution)/shard_map/all_to_all | solution.py:178
  231.1 0.9 gather_fusion.72
  232.1 1.1 fusion
  233.1 6.1 %reduce-scatter.2.cloned.1.call-done = bf16[96,2048]{1,0:T(8,128)(2,1)} async-done(((bf16[1536,2048]{1,0:T(8,128)(2,1)}), bf16[96,2048]{1,0:T(8,128)(2,1)}) %reduce-scatter.2.cloned.1.call-update) | async-done | bytes 393232 | tf_op jit(solution)/shard_map/reduce_scatter | solution.py:172
  239.3 2.8 %subtract_convert_fusion = (bf16[1,96,2048]{2,1,0:T(8,128)(2,1)}, f32[1,96,2048]{2,1,0:T(8,128)}, f32[1,96,2048]{2,1,0:T(8,128)}) fusion(bf16[1,96,2048]{2,1,0:T(8,128)(2,1)S(1)} %copy-done.2, f32[1,96,2048]{2,1,0:T(8,128)S(1)} %copy-done.1, bf16[96,2048]{1,0:T(8,128)(2,1)} %reduce-scatter.2.cloned.1.call-done, f32[1,96,2048]{2,1,0:T(8,128)} %get-tuple-element.380), kind=kLoop, calls=%fused_computation.170 | loop fusion | flops 2555904 | bytes 4325376 | tf_op jit(solution)/shard_map/convert_element_type | solution.py:25
  (58 shorter events, 6.7 us)
Async XLA Ops:
  7.2 71.3 %copy-start = (bf16[16,8,768]{2,1,0:T(8,128)(2,1)S(1)}, bf16[16,8,768]{2,1,0:T(8,128)(2,1)}, u32[]{:S(2)}) copy-start(bf16[16,8,768]{2,1,0:T(8,128)(2,1)} %param.47) | copy-start | bytes 589828
  7.2 13.7 %copy-start.6 = (s32[16,8]{0,1:T(8,128)S(1)}, s32[16,8]{0,1:T(8,128)}, u32[]{:S(2)}) copy-start(s32[16,8]{0,1:T(8,128)} %param.45) | copy-start | bytes 1540
  7.2 13.9 %copy-start.9 = (s32[64]{0:T(128)S(1)}, s32[64]{0:T(128)}, u32[]{:S(2)}) copy-start(s32[64]{0:T(128)} %param.50) | copy-start | bytes 772
  7.2 119.4 %all-gather.3.cloned.1.call-start = ((), (), s32[]{:S(2)}) async-start(), calls=%async_computation.8 | async-start | bytes 6684672 | tf_op jit(solution)/shard_map/all_gather | solution.py:137
  7.9 13.3 %copy-start.8 = (s32[64]{0:T(128)S(1)}, s32[64]{0:T(128)}, u32[]{:S(2)}) copy-start(s32[64]{0:T(128)} %param.49) | copy-start | bytes 772
  11.4 21.5 %all-to-all-start = ((bf16[32,1,96,128]{3,2,1,0:T(8,128)(2,1)}), bf16[32,1,96,128]{3,2,1,0:T(8,128)(2,1)S(1)}, u32[]{:S(2)}, u32[]{:S(2)}) async-start(bf16[32,1,96,128]{3,2,1,0:T(8,128)(2,1)} %bitcast.123), calls=%async_computation | async-start | bytes 1572864 | tf_op jit(solution)/shard_map/all_to_all | solution.py:129
  33.0 53.8 %copy-start.7 = (f32[16,8]{0,1:T(8,128)S(1)}, f32[16,8]{0,1:T(8,128)}, u32[]{:S(2)}) copy-start(f32[16,8]{0,1:T(8,128)} %param.46) | copy-start | bytes 1540
  33.0 53.9 %copy-start.5 = (bf16[16,2048]{1,0:T(8,128)(2,1)S(1)}, bf16[16,2048]{1,0:T(8,128)(2,1)}, u32[]{:S(2)}) copy-start(bf16[16,2048]{1,0:T(8,128)(2,1)} %param.48) | copy-start | bytes 196612
  33.7 44.1 %collective-permute-start.14 = (bf16[24,48,128]{2,1,0:T(8,128)(2,1)S(1)}, bf16[24,48,128]{2,1,0:T(8,128)(2,1)S(1)}, u32[]{:S(2)}, u32[]{:S(2)}) collective-permute-start(bf16[24,48,128]{2,1,0:T(8,128)(2,1)S(1)} %gather_fusion.28), channel_id=1, source_target_pairs={{0,32},{32,0},{1,33},{33,1},{2,34},{34,2},{3,35},{35,3},{4,36},{36... | collective-permute-start | bytes 884744 | tf_op jit(solution)/shard_map/cond/branch_14_fun/ppermute | solution.py:120
  80.3 14.6 %all-to-all-start.1 = ((bf16[32,8,768]{2,1,0:T(8,128)(2,1)}), bf16[32,8,768]{2,1,0:T(8,128)(2,1)S(1)}, u32[]{:S(2)}, u32[]{:S(2)}) async-start(bf16[32,8,768]{2,1,0:T(8,128)(2,1)} %bitcast.14), calls=%async_computation.1 | async-start | bytes 786432 | tf_op jit(solution)/shard_map/all_to_all | solution.py:148
  94.9 20.8 %all-to-all-start.2 = ((bf16[32,8,2048]{2,1,0:T(8,128)(2,1)}), bf16[32,8,2048]{2,1,0:T(8,128)(2,1)S(1)}, u32[]{:S(2)}, u32[]{:S(2)}) async-start(bf16[32,8,2048]{2,1,0:T(8,128)(2,1)} %bitcast.18), calls=%async_computation.2 | async-start | bytes 2097152 | tf_op jit(solution)/shard_map/all_to_all | solution.py:155
  101.1 138.2 %reduce-scatter.2.cloned.1.call-start = ((), (), s32[]{:S(2)}) async-start(), calls=%async_computation.7 | async-start | bytes 6684672 | tf_op jit(solution)/shard_map/reduce_scatter | solution.py:172
  126.6 12.9 %copy-start.3 = (bf16[256,768]{1,0:T(8,128)(2,1)S(1)}, bf16[256,768]{1,0:T(8,128)(2,1)}, u32[]{:S(2)}) copy-start(bf16[256,768]{1,0:T(8,128)(2,1)} %get-tuple-element.386) | copy-start | bytes 1179652
  126.6 12.9 %copy-start.4 = (bf16[256,768]{1,0:T(8,128)(2,1)S(1)}, bf16[256,768]{1,0:T(8,128)(2,1)}, u32[]{:S(2)}) copy-start(bf16[256,768]{1,0:T(8,128)(2,1)} %get-tuple-element.387) | copy-start | bytes 1179652
  132.1 58.6 %all-to-all-start.4 = ((bf16[32,8,768]{2,1,0:T(8,128)(2,1)}), bf16[32,8,768]{2,1,0:T(8,128)(2,1)S(1)}, u32[]{:S(2)}, u32[]{:S(2)}) async-start(bf16[32,8,768]{2,1,0:T(8,128)(2,1)} %fusion.38), calls=%async_computation.4 | async-start | bytes 786432 | tf_op jit(solution)/shard_map/all_to_all | solution.py:185
  145.7 44.4 %collective-permute-start.32 = (bf16[24,48,128]{2,1,0:T(8,128)(2,1)S(1)}, bf16[24,48,128]{2,1,0:T(8,128)(2,1)S(1)}, u32[]{:S(2)}, u32[]{:S(2)}) collective-permute-start(bf16[24,48,128]{2,1,0:T(8,128)(2,1)S(1)} %gather_fusion.64), channel_id=1, source_target_pairs={{0,32},{32,0},{1,33},{33,1},{2,34},{34,2},{3,35},{35,3},{4,36},{36... | collective-permute-start | bytes 884744 | tf_op jit(solution)/shard_map/cond/branch_14_fun/ppermute | solution.py:120
  210.0 21.1 %all-to-all-start.3 = ((bf16[32,8,2048]{2,1,0:T(8,128)(2,1)}), bf16[32,8,2048]{2,1,0:T(8,128)(2,1)S(1)}, u32[]{:S(2)}, u32[]{:S(2)}) async-start(bf16[32,8,2048]{2,1,0:T(8,128)(2,1)} %bitcast.20), calls=%async_computation.3 | async-start | bytes 2097152 | tf_op jit(solution)/shard_map/all_to_all | solution.py:178
  231.1 8.2 %copy-start.1 = (f32[1,96,2048]{2,1,0:T(8,128)S(1)}, f32[1,96,2048]{2,1,0:T(8,128)}, u32[]{:S(2)}) copy-start(f32[1,96,2048]{2,1,0:T(8,128)} %get-tuple-element.379) | copy-start | bytes 2359300
  231.1 8.2 %copy-start.2 = (bf16[1,96,2048]{2,1,0:T(8,128)(2,1)S(1)}, bf16[1,96,2048]{2,1,0:T(8,128)(2,1)}, u32[]{:S(2)}) copy-start(bf16[1,96,2048]{2,1,0:T(8,128)(2,1)} %get-tuple-element.378) | copy-start | bytes 1179652
Sparse Core Ops, SparseCore 0:
  10.1 116.3 all-gather.2
  129.4 109.8 reduce-scatter.1

commit v4 on v3

--- a/solution.py
+++ b/solution.py
@@ -132,8 +132,8 @@
     mine = spread_blocks.shape[1]
     spread_blocks = spread_blocks.reshape(plane, mine * rows_dp, LANES)
     cut = mine * rows_dp // 2
-    early_far = cross(spread_blocks[:, :cut])
-    hidden, upstream, _ = lax.optimization_barrier((hidden, upstream, early_far))
+    hidden, _ = lax.optimization_barrier((hidden, spread_blocks))
+    upstream, _ = lax.optimization_barrier((upstream, spread_blocks))
     full_weights = lax.all_gather(weights[0], ("zh", "dp"), axis=0, tiled=True)
 
     target = table_lookup(placement, route_ids.reshape(-1))
@@ -152,8 +152,11 @@
     send_grads = jnp.zeros((plane * slots, width), jnp.bfloat16)
     send_grads = send_grads.at[position].set(scaled.reshape(total_rows, width))
     send_grads = send_grads.reshape(plane, slots, width)
+
+    early_blocks, send_grads, _ = lax.optimization_barrier((spread_blocks[:, :cut], send_grads, got_hidden))
+    early_far = cross(early_blocks)
     got_grads = lax.all_to_all(send_grads, "p", split_axis=0, concat_axis=0, tiled=True)
-
+    got_grads, _ = lax.optimization_barrier((got_grads, early_far))
     flat_hidden = got_hidden.reshape(plane * slots, hidden_width)
     flat_grads = got_grads.reshape(plane * slots, width)
     half = (jnp.arange(plane * slots, dtype=jnp.int32) // capacity % 2)[:, None]
@@ -185,19 +188,10 @@
     back_grads = lax.all_to_all(
         row_grads.reshape(plane, slots, hidden_width), "p", split_axis=0, concat_axis=0, tiled=True
     )
-    expert_terms = back_terms.reshape(plane * slots, width)[position].reshape(
-        tokens_here, chosen, width
-    )
-    layer_out = jnp.sum(route_probs[..., None] * expert_terms.astype(jnp.float32), axis=1).astype(
-        jnp.bfloat16
-    )
-    hidden_grads = back_grads.reshape(plane * slots, hidden_width)[position].reshape(
-        tokens_here, chosen, hidden_width
-    )
-
     late_blocks, _, _ = lax.optimization_barrier((spread_blocks[:, cut:], terms, row_grads))
     late_far = cross(late_blocks)
     far = jnp.concatenate([early_far, late_far], axis=1).reshape(plane, mine, rows_dp, LANES)
+    far, back_terms = lax.optimization_barrier((far, back_terms))
     far = lax.all_to_all(far, "p", split_axis=0, concat_axis=0, tiled=True)
     old_half = my_half ^ flip_mine
     row_block = old_half * (hidden_width // rows_dp) + my_dp
@@ -207,6 +201,16 @@
     new_w, new_first, new_second = adam_update(
         weight_here, first_here, second_here, gradient[None].astype(jnp.float32)
     )
+    expert_terms = back_terms.reshape(plane * slots, width)[position].reshape(
+        tokens_here, chosen, width
+    )
+    layer_out = jnp.sum(route_probs[..., None] * expert_terms.astype(jnp.float32), axis=1).astype(
+        jnp.bfloat16
+    )
+    hidden_grads = back_grads.reshape(plane * slots, hidden_width)[position].reshape(
+        tokens_here, chosen, hidden_width
+    )
+
     return (layer_out, hidden_grads, new_w, new_first, new_second)
 
 

time: 250 us -> 238 us (0.952)
  blocking collectives: 19.2 us -> 0 us
  starting transfers between devices: 58.2 us -> 65.8 us
  waiting for transfers between devices: 113 us -> 110 us
    all_to_all x1 -> x0, blocking collectives: 19.2 us -> none  [shards(): far = lax.all_to_all(far, 'p', split_axis=0, concat_axis=0, tiled=True)]
    ppermute x2, waiting for transfers between devices: 66.3 us -> 50.1 us  [branch(): packed = lax.ppermute(packed, 'zh', [(0, 1), (1, 0)])]
    all_gather x1, waiting for transfers between devices: 6.3 us -> 20.3 us  [shards(): full_weights = lax.all_gather(weights[0], ('zh', 'dp'), axis=0, tiled=True)]
    all_to_all x1, waiting for transfers between devices: 12.1 us -> 0.01 us  [shards(): lax.all_to_all(send_grads, 'p', split_axis=0, concat_axis=0, tiled=True)]
    all_to_all x0 -> x1, starting transfers between devices: none -> 7.42 us  [shards(): far = lax.all_to_all(far, 'p', split_axis=0, concat_axis=0, tiled=True)]
    all_to_all x0 -> x1, waiting for transfers between devices: none -> 6.51 us  [shards(): far = lax.all_to_all(far, 'p', split_axis=0, concat_axis=0, tiled=True)]
    reduce_scatter x1, waiting for transfers between devices: 6.13 us -> 8.76 us  [shards(): lax.psum_scatter(partial, ('zh', 'dp'), scatter_dimension=0, tiled=True)]
    all_to_all x1, waiting for transfers between devices: 6.55 us -> 9.16 us  [shards(): lax.all_to_all(terms.reshape(plane, slots, width), 'p', split_axis=0, con...]
  transfers between devices with their start and end apart: 9 -> 10, of which waited for: 8 -> 8; matrix products, arithmetic and copies ran while one was open for 13% -> 14% of each run, Pallas kernels for 3% -> 3%
where the time goes in v4:
time: 238 us; the launch traced here: 236 us
  waiting for transfers between devices  110 us (46%)
  starting transfers between devices  65.8 us (28%)
  between operations  15.6 us (7%)
  matrix products  14.6 us (6%)
  other arithmetic  13.2 us (6%)
  local copies, waits for them, and re-layouts  8.66 us (4%)
  Pallas kernels  8.17 us (3%)
    ppermute x2, waiting for transfers between devices, branch(): packed = lax.ppermute(packed, 'zh', [(0, 1), (1, 0)])  50.1 us
    ppermute x2, starting transfers between devices, branch(): packed = lax.ppermute(packed, 'zh', [(0, 1), (1, 0)])  22.4 us
    all_gather x1, waiting for transfers between devices, shards(): full_weights = lax.all_gather(weights[0], ('zh', 'dp'), axis=0, tiled=True)  20.3 us
    all_to_all x1, waiting for transfers between devices, shards(): lax.all_to_all(moment_blocks.reshape(plane, -1, rows_dp, LANES), 'p', spl...  11 us
    all_to_all x1, starting transfers between devices, shards(): lax.all_to_all(moment_blocks.reshape(plane, -1, rows_dp, LANES), 'p', spl...  9.58 us
    all_to_all x1, waiting for transfers between devices, shards(): lax.all_to_all(terms.reshape(plane, slots, width), 'p', split_axis=0, con...  9.16 us
    reduce_scatter x1, waiting for transfers between devices, shards(): lax.psum_scatter(partial, ('zh', 'dp'), scatter_dimension=0, tiled=True)  8.76 us
    all_to_all x1, starting transfers between devices, shards(): far = lax.all_to_all(far, 'p', split_axis=0, concat_axis=0, tiled=True)  7.42 us
  transfers between devices with their start and end apart: 10, of which 8 were waited for; matrix products, arithmetic and copies ran while one was open for 14% of the time, Pallas kernels for 3%

profile of v4, /device:TPU:6, one launch (start us, length us, event | category | flops | bytes accessed | tf_op | source)
XLA Modules:
  0.0 236.5 jit_solution(3844077769689710739)
XLA Ops:
  7.9 3.5 %shard_map.128 = bf16[2,16,96,128]{3,2,1,0:T(8,128)(2,1)} custom-call(f32[1,96,2048]{2,1,0:T(8,128)} %first_ref.3, f32[1,96,2048]{2,1,0:T(8,128)} %second_ref.3), custom_call_target="tpu_custom_call" | custom-call | tf_op jit(solution)/shard_map/pallas_call | solution.py:40
  11.4 9.6 %all-to-all-start = ((bf16[32,1,96,128]{3,2,1,0:T(8,128)(2,1)}), bf16[32,1,96,128]{3,2,1,0:T(8,128)(2,1)S(1)}, u32[]{:S(2)}, u32[]{:S(2)}) async-start(bf16[32,1,96,128]{3,2,1,0:T(8,128)(2,1)} %bitcast.123), calls=%async_computation | async-start | bytes 1572864 | tf_op jit(solution)/shard_map/all_to_all | solution.py:129
  22.1 11.0 %all-to-all-done = bf16[32,1,96,128]{3,2,1,0:T(8,128)(2,1)S(1)} async-done(((bf16[32,1,96,128]{3,2,1,0:T(8,128)(2,1)}), bf16[32,1,96,128]{3,2,1,0:T(8,128)(2,1)S(1)}, u32[]{:S(2)}, u32[]{:S(2)}) %all-to-all-start) | async-done | bytes 786464 | tf_op jit(solution)/shard_map/all_to_all | solution.py:129
  33.1 1.9 scatter_custom_fusion.1
  35.0 6.4 %all-to-all-start.1 = ((bf16[32,8,768]{2,1,0:T(8,128)(2,1)}), bf16[32,8,768]{2,1,0:T(8,128)(2,1)S(1)}, u32[]{:S(2)}, u32[]{:S(2)}) async-start(bf16[32,8,768]{2,1,0:T(8,128)(2,1)} %bitcast.16), calls=%async_computation.1 | async-start | bytes 786432 | tf_op jit(solution)/shard_map/all_to_all | solution.py:148
  43.4 2.5 %scatter_custom_fusion = bf16[256,2048]{1,0:T(8,128)(2,1)} fusion(s32[128]{0:T(128)S(1)} %fusion.29, f32[16,2048]{1,0:T(8,128)S(1)} %convert_element_type.193, f32[128]{0:T(128)S(1)} %mul.98, bf16[]{:T(256)} %constant.164.clone.1), kind=kCustom, calls=%fused_computation.171 | custom fusion | flops 524288 | bytes 1180162 | tf_op jit(solution)/shard_map/scatter | solution.py:153
  46.0 3.5 %all-to-all-done.1 = bf16[32,8,768]{2,1,0:T(8,128)(2,1)S(1)} async-done(((bf16[32,8,768]{2,1,0:T(8,128)(2,1)}), bf16[32,8,768]{2,1,0:T(8,128)(2,1)S(1)}, u32[]{:S(2)}, u32[]{:S(2)}) %all-to-all-start.1) | async-done | bytes 393248 | tf_op jit(solution)/shard_map/all_to_all | solution.py:148
  49.5 6.1 %all-to-all-start.2 = ((bf16[32,8,2048]{2,1,0:T(8,128)(2,1)}), bf16[32,8,2048]{2,1,0:T(8,128)(2,1)S(1)}, u32[]{:S(2)}, u32[]{:S(2)}) async-start(bf16[32,8,2048]{2,1,0:T(8,128)(2,1)} %bitcast.14), calls=%async_computation.2 | async-start | bytes 2097152 | tf_op jit(solution)/shard_map/all_to_all | solution.py:158
  56.5 37.7 %conditional.2 = (bf16[32,48,128]{2,1,0:T(8,128)(2,1)S(1)}) conditional(s32[]{:T(128)} %clamp.4, (s32[32]{0:T(128)S(1)}, bf16[32,48,128]{2,1,0:T(8,128)(2,1)S(1)}, s32[32]{0:T(128)S(1)}) %tuple.126, (s32[32]{0:T(128)S(1)}, bf16[32,48,128]{2,1,0:T(8,128)(2,1)S(1)}, s32[32]{0:T(128)S(1)}) %tuple.126, (s32[32]{0:T(128)S(1)}, ...), branch_computations={%region_7.8_spmd, %region_8.9_spmd, %region_9.10_spmd, %region_10.... | conditional | flops 2048 | bytes 3154480 | solution.py:126
  57.1 13.8 %collective-permute-start.9 = (bf16[18,48,128]{2,1,0:T(8,128)(2,1)S(1)}, bf16[18,48,128]{2,1,0:T(8,128)(2,1)S(1)}, u32[]{:S(2)}, u32[]{:S(2)}) collective-permute-start(bf16[18,48,128]{2,1,0:T(8,128)(2,1)S(1)} %gather_fusion.18), channel_id=1, source_target_pairs={{0,32},{32,0},{1,33},{33,1},{2,34},{34,2},{3,35},{35,3},{4,36},{36... | collective-permute-start | bytes 663560 | tf_op jit(solution)/shard_map/cond/branch_9_fun/ppermute | solution.py:120
  70.9 22.4 %collective-permute-done.9 = bf16[18,48,128]{2,1,0:T(8,128)(2,1)S(1)} collective-permute-done((bf16[18,48,128]{2,1,0:T(8,128)(2,1)S(1)}, bf16[18,48,128]{2,1,0:T(8,128)(2,1)S(1)}, u32[]{:S(2)}, u32[]{:S(2)}) %collective-permute-start.9) | collective-permute-done | bytes 221216 | tf_op jit(solution)/shard_map/cond/branch_9_fun/ppermute | solution.py:120
  94.2 1.1 bitcast_select_fusion.3
  95.2 4.5 %convolution_convert_fusion = bf16[1536,2048]{1,0:T(8,128)(2,1)} fusion(bf16[32,8,2048]{2,1,0:T(8,128)(2,1)S(1)} %all-to-all-done.2, bf16[256,768]{1,0:T(8,128)(2,1)S(1)} %get-tuple-element.399, bf16[256,768]{1,0:T(8,128)(2,1)S(1)} %get-tuple-element.398), kind=kOutput, calls=%fused_computation.148 | convolution fusion | flops 1615331328 | bytes 8126464 | tf_op jit(solution)/shard_map/dot_general | solution.py:172
  99.8 20.3 %all-gather.3.cloned.1.call-done = bf16[1,1536,2048]{2,1,0:T(8,128)(2,1)} async-done(((bf16[1,96,2048]{2,1,0:T(8,128)(2,1)}), bf16[1,1536,2048]{2,1,0:T(8,128)(2,1)}) %all-gather.3.cloned.1.call-update) | async-done | bytes 6291472 | tf_op jit(solution)/shard_map/all_gather | solution.py:137
  120.0 5.6 %convolution_convert_fusion.2 = bf16[256,2048]{1,0:T(8,128)(2,1)} fusion(bf16[1536,2048]{1,0:T(8,128)(2,1)} %bitcast.118, bf16[256,768]{1,0:T(8,128)(2,1)S(1)} %copy-done.3, bf16[256,768]{1,0:T(8,128)(2,1)S(1)} %copy-done.2), kind=kOutput, calls=%fused_computation.150 | convolution fusion | flops 1612709888 | bytes 8126464 | tf_op jit(solution)/shard_map/dot_general | solution.py:180
  125.6 7.4 %all-to-all-start.3 = ((bf16[32,8,2048]{2,1,0:T(8,128)(2,1)}), bf16[32,8,2048]{2,1,0:T(8,128)(2,1)S(1)}, u32[]{:S(2)}, u32[]{:S(2)}) async-start(bf16[32,8,2048]{2,1,0:T(8,128)(2,1)} %bitcast.124), calls=%async_computation.3 | async-start | bytes 2097152 | tf_op jit(solution)/shard_map/all_to_all | solution.py:181
  133.0 4.6 %convolution_convert_fusion.1 = bf16[256,1536]{1,0:T(8,128)(2,1)S(1)} fusion(bf16[1536,2048]{1,0:T(8,128)(2,1)} %bitcast.119, bf16[32,8,2048]{2,1,0:T(8,128)(2,1)S(1)} %all-to-all-done.2), kind=kOutput, calls=%fused_computation.149 | convolution fusion | flops 1611005952 | bytes 8126464 | tf_op jit(solution)/shard_map/dot_general | solution.py:184
  138.5 9.2 %all-to-all-done.3 = bf16[32,8,2048]{2,1,0:T(8,128)(2,1)S(1)} async-done(((bf16[32,8,2048]{2,1,0:T(8,128)(2,1)}), bf16[32,8,2048]{2,1,0:T(8,128)(2,1)S(1)}, u32[]{:S(2)}, u32[]{:S(2)}) %all-to-all-start.3) | async-done | bytes 1048608 | tf_op jit(solution)/shard_map/all_to_all | solution.py:181
  147.6 6.5 %all-to-all-start.4 = ((bf16[32,8,768]{2,1,0:T(8,128)(2,1)}), bf16[32,8,768]{2,1,0:T(8,128)(2,1)S(1)}, u32[]{:S(2)}, u32[]{:S(2)}) async-start(bf16[32,8,768]{2,1,0:T(8,128)(2,1)} %fusion.38), calls=%async_computation.4 | async-start | bytes 786432 | tf_op jit(solution)/shard_map/all_to_all | solution.py:188
  154.2 37.6 %conditional.3 = (bf16[32,48,128]{2,1,0:T(8,128)(2,1)S(1)}) conditional(s32[]{:T(128)} %clamp.4, (s32[32]{0:T(128)S(1)}, bf16[32,48,128]{2,1,0:T(8,128)(2,1)S(1)}, s32[32]{0:T(128)S(1)}) %tuple.130, (s32[32]{0:T(128)S(1)}, bf16[32,48,128]{2,1,0:T(8,128)(2,1)S(1)}, s32[32]{0:T(128)S(1)}) %tuple.130, (s32[32]{0:T(128)S(1)}, ...), branch_computations={%region_26.27_spmd, %region_27.28_spmd, %region_28.29_spmd, %regio... | conditional | flops 2048 | bytes 3154480 | solution.py:126
  154.8 8.6 %collective-permute-start.27 = (bf16[18,48,128]{2,1,0:T(8,128)(2,1)S(1)}, bf16[18,48,128]{2,1,0:T(8,128)(2,1)S(1)}, u32[]{:S(2)}, u32[]{:S(2)}) collective-permute-start(bf16[18,48,128]{2,1,0:T(8,128)(2,1)S(1)} %gather_fusion.54), channel_id=1, source_target_pairs={{0,32},{32,0},{1,33},{33,1},{2,34},{34,2},{3,35},{35,3},{4,36},{36... | collective-permute-start | bytes 663560 | tf_op jit(solution)/shard_map/cond/branch_9_fun/ppermute | solution.py:120
  163.4 27.7 %collective-permute-done.27 = bf16[18,48,128]{2,1,0:T(8,128)(2,1)S(1)} collective-permute-done((bf16[18,48,128]{2,1,0:T(8,128)(2,1)S(1)}, bf16[18,48,128]{2,1,0:T(8,128)(2,1)S(1)}, u32[]{:S(2)}, u32[]{:S(2)}) %collective-permute-start.27) | collective-permute-done | bytes 221216 | tf_op jit(solution)/shard_map/cond/branch_9_fun/ppermute | solution.py:120
  191.8 0.9 maximum_bitcast_fusion
  192.7 7.4 %all-to-all-start.5 = ((bf16[32,1,96,128]{3,2,1,0:T(8,128)(2,1)}), bf16[32,1,96,128]{3,2,1,0:T(8,128)(2,1)S(1)}, u32[]{:S(2)}, u32[]{:S(2)}) async-start(bf16[32,1,96,128]{3,2,1,0:T(8,128)(2,1)} %maximum_bitcast_fusion), calls=%async_computation.5 | async-start | bytes 1572864 | tf_op jit(solution)/shard_map/all_to_all | solution.py:195
  200.8 1.3 pad_add_fusion.where_ref
  202.0 1.5 gather_fusion.73
  203.6 0.9 gather_fusion.72
  204.5 1.1 fusion
  205.6 6.5 %all-to-all-done.5 = bf16[32,1,96,128]{3,2,1,0:T(8,128)(2,1)S(1)} async-done(((bf16[32,1,96,128]{3,2,1,0:T(8,128)(2,1)}), bf16[32,1,96,128]{3,2,1,0:T(8,128)(2,1)S(1)}, u32[]{:S(2)}, u32[]{:S(2)}) %all-to-all-start.5) | async-done | bytes 786464 | tf_op jit(solution)/shard_map/all_to_all | solution.py:195
  213.0 4.7 %shard_map.129 = (bf16[1,96,2048]{2,1,0:T(8,128)(2,1)}, f32[1,96,2048]{2,1,0:T(8,128)}, f32[1,96,2048]{2,1,0:T(8,128)}) custom-call(s32[2]{0:T(128)} %pad_add_fusion.where_ref, bf16[1536,2048]{1,0:T(8,128)(2,1)} %bitcast.120, f32[1,96,2048]{2,1,0:T(8,128)} %first_ref.3, f32[1,96,2048]{2,1,0:T(8,128)} %second_ref.3, bf16[2,16,96,128]{3,2,1,0:T(8,128)(2,1)} %bitcast.121), custom_call_target="tpu_custom_call" | custom-call | tf_op jit(solution)/shard_map/pallas_call | solution.py:76
  217.7 8.8 %reduce-scatter.2.cloned.1.call-done = bf16[96,2048]{1,0:T(8,128)(2,1)} async-done(((bf16[1536,2048]{1,0:T(8,128)(2,1)}), bf16[96,2048]{1,0:T(8,128)(2,1)}) %reduce-scatter.2.cloned.1.call-update) | async-done | bytes 393232 | tf_op jit(solution)/shard_map/reduce_scatter | solution.py:175
  226.4 3.2 %subtract_convert_fusion = (bf16[1,96,2048]{2,1,0:T(8,128)(2,1)}, f32[1,96,2048]{2,1,0:T(8,128)}, f32[1,96,2048]{2,1,0:T(8,128)}) fusion(bf16[1,96,2048]{2,1,0:T(8,128)(2,1)} %get-tuple-element.388, f32[1,96,2048]{2,1,0:T(8,128)} %get-tuple-element.389, bf16[96,2048]{1,0:T(8,128)(2,1)} %reduce-scatter.2.cloned.1.call-done, f32[1,96,2048]{2,1,0:T(8,128)} %get-tuple-element.390), kind=kLoop, calls=%fused_computation.170 | loop fusion | flops 2555904 | bytes 4325376 | tf_op jit(solution)/shard_map/convert_element_type | solution.py:25
  (57 shorter events, 8.2 us)
Async XLA Ops:
  7.2 26.0 %copy-start = (bf16[16,8,768]{2,1,0:T(8,128)(2,1)S(1)}, bf16[16,8,768]{2,1,0:T(8,128)(2,1)}, u32[]{:S(2)}) copy-start(bf16[16,8,768]{2,1,0:T(8,128)(2,1)} %param.47) | copy-start | bytes 589828
  7.2 13.9 %copy-start.5 = (s32[16,8]{0,1:T(8,128)S(1)}, s32[16,8]{0,1:T(8,128)}, u32[]{:S(2)}) copy-start(s32[16,8]{0,1:T(8,128)} %param.45) | copy-start | bytes 1540
  7.2 14.0 %copy-start.8 = (s32[64]{0:T(128)S(1)}, s32[64]{0:T(128)}, u32[]{:S(2)}) copy-start(s32[64]{0:T(128)} %param.50) | copy-start | bytes 772
  7.2 112.8 %all-gather.3.cloned.1.call-start = ((), (), s32[]{:S(2)}) async-start(), calls=%async_computation.8 | async-start | bytes 6684672 | tf_op jit(solution)/shard_map/all_gather | solution.py:137
  7.9 13.4 %copy-start.7 = (s32[64]{0:T(128)S(1)}, s32[64]{0:T(128)}, u32[]{:S(2)}) copy-start(s32[64]{0:T(128)} %param.49) | copy-start | bytes 772
  11.4 29.9 %copy-start.6 = (f32[16,8]{0,1:T(8,128)S(1)}, f32[16,8]{0,1:T(8,128)}, u32[]{:S(2)}) copy-start(f32[16,8]{0,1:T(8,128)} %param.46) | copy-start | bytes 1540
  11.4 32.0 %copy-start.4 = (bf16[16,2048]{1,0:T(8,128)(2,1)S(1)}, bf16[16,2048]{1,0:T(8,128)(2,1)}, u32[]{:S(2)}) copy-start(bf16[16,2048]{1,0:T(8,128)(2,1)} %param.48) | copy-start | bytes 196612
  11.4 21.7 %all-to-all-start = ((bf16[32,1,96,128]{3,2,1,0:T(8,128)(2,1)}), bf16[32,1,96,128]{3,2,1,0:T(8,128)(2,1)S(1)}, u32[]{:S(2)}, u32[]{:S(2)}) async-start(bf16[32,1,96,128]{3,2,1,0:T(8,128)(2,1)} %bitcast.123), calls=%async_computation | async-start | bytes 1572864 | tf_op jit(solution)/shard_map/all_to_all | solution.py:129
  35.0 14.5 %all-to-all-start.1 = ((bf16[32,8,768]{2,1,0:T(8,128)(2,1)}), bf16[32,8,768]{2,1,0:T(8,128)(2,1)S(1)}, u32[]{:S(2)}, u32[]{:S(2)}) async-start(bf16[32,8,768]{2,1,0:T(8,128)(2,1)} %bitcast.16), calls=%async_computation.1 | async-start | bytes 786432 | tf_op jit(solution)/shard_map/all_to_all | solution.py:148
  49.5 45.8 %all-to-all-start.2 = ((bf16[32,8,2048]{2,1,0:T(8,128)(2,1)}), bf16[32,8,2048]{2,1,0:T(8,128)(2,1)S(1)}, u32[]{:S(2)}, u32[]{:S(2)}) async-start(bf16[32,8,2048]{2,1,0:T(8,128)(2,1)} %bitcast.14), calls=%async_computation.2 | async-start | bytes 2097152 | tf_op jit(solution)/shard_map/all_to_all | solution.py:158
  55.6 170.8 %reduce-scatter.2.cloned.1.call-start = ((), (), s32[]{:S(2)}) async-start(), calls=%async_computation.7 | async-start | bytes 6684672 | tf_op jit(solution)/shard_map/reduce_scatter | solution.py:175
  57.1 36.2 %collective-permute-start.9 = (bf16[18,48,128]{2,1,0:T(8,128)(2,1)S(1)}, bf16[18,48,128]{2,1,0:T(8,128)(2,1)S(1)}, u32[]{:S(2)}, u32[]{:S(2)}) collective-permute-start(bf16[18,48,128]{2,1,0:T(8,128)(2,1)S(1)} %gather_fusion.18), channel_id=1, source_target_pairs={{0,32},{32,0},{1,33},{33,1},{2,34},{34,2},{3,35},{35,3},{4,36},{36... | collective-permute-start | bytes 663560 | tf_op jit(solution)/shard_map/cond/branch_9_fun/ppermute | solution.py:120
  99.7 20.3 %copy-start.2 = (bf16[256,768]{1,0:T(8,128)(2,1)S(1)}, bf16[256,768]{1,0:T(8,128)(2,1)}, u32[]{:S(2)}) copy-start(bf16[256,768]{1,0:T(8,128)(2,1)} %get-tuple-element.396) | copy-start | bytes 1179652
  99.7 20.3 %copy-start.3 = (bf16[256,768]{1,0:T(8,128)(2,1)S(1)}, bf16[256,768]{1,0:T(8,128)(2,1)}, u32[]{:S(2)}) copy-start(bf16[256,768]{1,0:T(8,128)(2,1)} %get-tuple-element.397) | copy-start | bytes 1179652
  125.6 22.0 %all-to-all-start.3 = ((bf16[32,8,2048]{2,1,0:T(8,128)(2,1)}), bf16[32,8,2048]{2,1,0:T(8,128)(2,1)S(1)}, u32[]{:S(2)}, u32[]{:S(2)}) async-start(bf16[32,8,2048]{2,1,0:T(8,128)(2,1)} %bitcast.124), calls=%async_computation.3 | async-start | bytes 2097152 | tf_op jit(solution)/shard_map/all_to_all | solution.py:181
  147.6 45.1 %all-to-all-start.4 = ((bf16[32,8,768]{2,1,0:T(8,128)(2,1)}), bf16[32,8,768]{2,1,0:T(8,128)(2,1)S(1)}, u32[]{:S(2)}, u32[]{:S(2)}) async-start(bf16[32,8,768]{2,1,0:T(8,128)(2,1)} %fusion.38), calls=%async_computation.4 | async-start | bytes 786432 | tf_op jit(solution)/shard_map/all_to_all | solution.py:188
  154.8 36.3 %collective-permute-start.27 = (bf16[18,48,128]{2,1,0:T(8,128)(2,1)S(1)}, bf16[18,48,128]{2,1,0:T(8,128)(2,1)S(1)}, u32[]{:S(2)}, u32[]{:S(2)}) collective-permute-start(bf16[18,48,128]{2,1,0:T(8,128)(2,1)S(1)} %gather_fusion.54), channel_id=1, source_target_pairs={{0,32},{32,0},{1,33},{33,1},{2,34},{34,2},{3,35},{35,3},{4,36},{36... | collective-permute-start | bytes 663560 | tf_op jit(solution)/shard_map/cond/branch_9_fun/ppermute | solution.py:120
  192.7 19.4 %all-to-all-start.5 = ((bf16[32,1,96,128]{3,2,1,0:T(8,128)(2,1)}), bf16[32,1,96,128]{3,2,1,0:T(8,128)(2,1)S(1)}, u32[]{:S(2)}, u32[]{:S(2)}) async-start(bf16[32,1,96,128]{3,2,1,0:T(8,128)(2,1)} %maximum_bitcast_fusion), calls=%async_computation.5 | async-start | bytes 1572864 | tf_op jit(solution)/shard_map/all_to_all | solution.py:195
  212.1 0.9 copy-start.1
Sparse Core Ops, SparseCore 0:
  10.1 109.8 all-gather.2
  122.9 103.5 reduce-scatter.1

commit v5 on v4

--- a/solution.py
+++ b/solution.py
@@ -46,22 +46,32 @@
     )(first, second)
 
 
-def home_kernel(where_ref, weight_ref, first_ref, second_ref, far_ref, w_ref, m_ref, v_ref):
+def home_kernel(
+    where_ref, weight_ref, first_ref, second_ref, early_ref, late_ref, w_ref, m_ref, v_ref
+):
     moved = where_ref[1] == 1
     w_ref[0] = weight_ref[...]
-    for block in range(far_ref.shape[1]):
+    cut = early_ref.shape[2]
+    for block in range(early_ref.shape[1]):
         columns = pl.ds(block * LANES, LANES)
-        first = jnp.where(moved, far_ref[0, block].astype(jnp.float32), first_ref[0, :, columns])
-        second = jnp.where(moved, far_ref[1, block].astype(jnp.float32), second_ref[0, :, columns])
-        m_ref[0, :, columns] = decay_one * first
-        v_ref[0, :, columns] = decay_two * second
-
-
-def state_at_home(row_block, moved, full_weights, first, second, far):
+        for rows, far_ref in ((pl.ds(0, cut), early_ref), (pl.ds(cut, late_ref.shape[2]), late_ref)):
+            far_first = far_ref[0, block].astype(jnp.float32)
+            far_second = far_ref[1, block].astype(jnp.float32)
+            first = jnp.where(moved, far_first, first_ref[0, rows, columns])
+            second = jnp.where(moved, far_second, second_ref[0, rows, columns])
+            m_ref[0, rows, columns] = decay_one * first
+            v_ref[0, rows, columns] = decay_two * second
+
+
+def state_at_home(row_block, moved, full_weights, first, second, early, late):
     _, rows, width = first.shape
     blocks = width // LANES
     step = STEP if blocks % STEP == 0 else 1
     state = pl.BlockSpec((1, rows, step * LANES), lambda i, where: (0, 0, i))
+
+    def far(part):
+        return pl.BlockSpec((2, step, part.shape[2], LANES), lambda i, where: (0, i, 0, 0))
+
     grid_spec = pltpu.PrefetchScalarGridSpec(
         num_scalar_prefetch=1,
         grid=(blocks // step,),
@@ -69,7 +79,8 @@
             pl.BlockSpec((rows, step * LANES), lambda i, where: (where[0], i)),
             state,
             state,
-            pl.BlockSpec((2, step, rows, LANES), lambda i, where: (0, i, 0, 0)),
+            far(early),
+            far(late),
         ],
         out_specs=[state, state, state],
     )
@@ -81,7 +92,7 @@
             jax.ShapeDtypeStruct(first.shape, jnp.float32),
             jax.ShapeDtypeStruct(first.shape, jnp.float32),
         ],
-    )(jnp.stack([row_block, moved]), full_weights, first, second, far)
+    )(jnp.stack([row_block, moved]), full_weights, first, second, early, late)
 
 
 def table_lookup(lookup_table, positions):
@@ -129,9 +140,8 @@
     spread_blocks = lax.all_to_all(
         moment_blocks.reshape(plane, -1, rows_dp, LANES), "p", split_axis=0, concat_axis=0, tiled=True
     )
-    mine = spread_blocks.shape[1]
-    spread_blocks = spread_blocks.reshape(plane, mine * rows_dp, LANES)
-    cut = mine * rows_dp // 2
+    spread_blocks = spread_blocks.reshape(plane, rows_dp, LANES)
+    cut = rows_dp * 4 // 12 // 8 * 8
     hidden, _ = lax.optimization_barrier((hidden, spread_blocks))
     upstream, _ = lax.optimization_barrier((upstream, spread_blocks))
     full_weights = lax.all_gather(weights[0], ("zh", "dp"), axis=0, tiled=True)
@@ -175,7 +185,11 @@
     gradient = lax.psum_scatter(
         partial, ("zh", "dp"), scatter_dimension=0, tiled=True
     )
-    full_weights, _ = lax.optimization_barrier((full_weights, partial))
+    early_far, _ = lax.optimization_barrier((early_far, partial))
+    early_home = lax.all_to_all(early_far, "p", split_axis=0, concat_axis=0, tiled=True)
+    late_blocks, full_weights, _ = lax.optimization_barrier((spread_blocks[:, cut:], full_weights, early_home))
+    late_far = cross(late_blocks)
+    full_weights, _ = lax.optimization_barrier((full_weights, late_far))
 
     terms = jnp.dot(spread, full_weights, preferred_element_type=jnp.float32).astype(jnp.bfloat16)
     back_terms = lax.all_to_all(
@@ -188,15 +202,18 @@
     back_grads = lax.all_to_all(
         row_grads.reshape(plane, slots, hidden_width), "p", split_axis=0, concat_axis=0, tiled=True
     )
-    late_blocks, _, _ = lax.optimization_barrier((spread_blocks[:, cut:], terms, row_grads))
-    late_far = cross(late_blocks)
-    far = jnp.concatenate([early_far, late_far], axis=1).reshape(plane, mine, rows_dp, LANES)
-    far, back_terms = lax.optimization_barrier((far, back_terms))
-    far = lax.all_to_all(far, "p", split_axis=0, concat_axis=0, tiled=True)
+    late_far, _ = lax.optimization_barrier((late_far, back_grads))
+    late_home = lax.all_to_all(late_far, "p", split_axis=0, concat_axis=0, tiled=True)
     old_half = my_half ^ flip_mine
     row_block = old_half * (hidden_width // rows_dp) + my_dp
     weight_here, first_here, second_here = state_at_home(
-        row_block, flip_mine, full_weights, moment1, moment2, far.reshape(moment_blocks.shape)
+        row_block,
+        flip_mine,
+        full_weights,
+        moment1,
+        moment2,
+        early_home.reshape(2, plane // 2, cut, LANES),
+        late_home.reshape(2, plane // 2, rows_dp - cut, LANES),
     )
     new_w, new_first, new_second = adam_update(
         weight_here, first_here, second_here, gradient[None].astype(jnp.float32)

time: 238 us -> 229 us (0.962)
  waiting for transfers between devices: 110 us -> 80 us
  blocking collectives: 0 us -> 19.9 us
  local copies, waits for them, and re-layouts: 8.66 us -> 11.3 us
    all_to_all x0 -> x1, blocking collectives: none -> 19.9 us  [shards(): lax.all_to_all(row_grads.reshape(plane, slots, hidden_width), 'p', split_...]
    all_gather x1, waiting for transfers between devices: 20.3 us -> 6.93 us  [shards(): full_weights = lax.all_gather(weights[0], ('zh', 'dp'), axis=0, tiled=True)]
    ppermute x2, waiting for transfers between devices: 50.1 us -> 37.6 us  [branch(): packed = lax.ppermute(packed, 'zh', [(0, 1), (1, 0)])]
    all_to_all x2, waiting for transfers between devices: 6.51 us -> 10.8 us  [the longest x1 6.95 us: shards(): lax.all_to_all(early_far, 'p', split_axis=0, concat_axis=0, tiled=True)]
    all_to_all x1, waiting for transfers between devices: 9.16 us -> 6.59 us  [shards(): lax.all_to_all(terms.reshape(plane, slots, width), 'p', split_axis=0, con...]
    reduce_scatter x1, waiting for transfers between devices: 8.76 us -> 6.23 us  [shards(): lax.psum_scatter(partial, ('zh', 'dp'), scatter_dimension=0, tiled=True)]
  transfers between devices with their start and end apart: 10 -> 10, of which waited for: 8 -> 9; matrix products, arithmetic and copies ran while one was open for 14% -> 16% of each run, Pallas kernels for 3% -> 4%
where the time goes in v5:
time: 229 us; the launch traced here: 227 us
  waiting for transfers between devices  80 us (35%)
  starting transfers between devices  64.2 us (28%)
  blocking collectives  19.9 us (9%)
  between operations  15.6 us (7%)
  matrix products  14.8 us (6%)
  other arithmetic  12.8 us (6%)
  local copies, waits for them, and re-layouts  11.3 us (5%)
  Pallas kernels  8.17 us (4%)
    ppermute x2, waiting for transfers between devices, branch(): packed = lax.ppermute(packed, 'zh', [(0, 1), (1, 0)])  37.6 us
    ppermute x2, starting transfers between devices, branch(): packed = lax.ppermute(packed, 'zh', [(0, 1), (1, 0)])  22.4 us
    all_to_all x1, blocking collectives, shards(): lax.all_to_all(row_grads.reshape(plane, slots, hidden_width), 'p', split_...  19.9 us
    all_to_all x1, waiting for transfers between devices, shards(): lax.all_to_all(moment_blocks.reshape(plane, -1, rows_dp, LANES), 'p', spl...  9.92 us
    all_to_all x1, starting transfers between devices, shards(): lax.all_to_all(moment_blocks.reshape(plane, -1, rows_dp, LANES), 'p', spl...  9.45 us
    all_to_all x1, starting transfers between devices, shards(): lax.all_to_all(early_far, 'p', split_axis=0, concat_axis=0, tiled=True)  7.39 us
    all_to_all x1, waiting for transfers between devices, shards(): lax.all_to_all(early_far, 'p', split_axis=0, concat_axis=0, tiled=True)  6.95 us
    all_gather x1, waiting for transfers between devices, shards(): full_weights = lax.all_gather(weights[0], ('zh', 'dp'), axis=0, tiled=True)  6.93 us
  transfers between devices with their start and end apart: 10, of which 9 were waited for; matrix products, arithmetic and copies ran while one was open for 16% of the time, Pallas kernels for 4%

profile of v5, /device:TPU:6, one launch (start us, length us, event | category | flops | bytes accessed | tf_op | source)
XLA Modules:
  0.0 226.8 jit_solution(4462349037788650180)
XLA Ops:
  7.9 3.5 %shard_map.128 = bf16[2,16,96,128]{3,2,1,0:T(8,128)(2,1)} custom-call(f32[1,96,2048]{2,1,0:T(8,128)} %first_ref.3, f32[1,96,2048]{2,1,0:T(8,128)} %second_ref.3), custom_call_target="tpu_custom_call" | custom-call | tf_op jit(solution)/shard_map/pallas_call | solution.py:40
  11.4 9.4 %all-to-all-start = ((bf16[32,1,96,128]{3,2,1,0:T(8,128)(2,1)}), bf16[32,1,96,128]{3,2,1,0:T(8,128)(2,1)S(1)}, u32[]{:S(2)}, u32[]{:S(2)}) async-start(bf16[32,1,96,128]{3,2,1,0:T(8,128)(2,1)} %bitcast.123), calls=%async_computation | async-start | bytes 1572864 | tf_op jit(solution)/shard_map/all_to_all | solution.py:140
  23.0 9.9 %all-to-all-done = bf16[32,1,96,128]{3,2,1,0:T(8,128)(2,1)S(1)} async-done(((bf16[32,1,96,128]{3,2,1,0:T(8,128)(2,1)}), bf16[32,1,96,128]{3,2,1,0:T(8,128)(2,1)S(1)}, u32[]{:S(2)}, u32[]{:S(2)}) %all-to-all-start) | async-done | bytes 786464 | tf_op jit(solution)/shard_map/all_to_all | solution.py:140
  33.0 1.9 scatter_custom_fusion
  34.8 6.4 %all-to-all-start.1 = ((bf16[32,8,768]{2,1,0:T(8,128)(2,1)}), bf16[32,8,768]{2,1,0:T(8,128)(2,1)S(1)}, u32[]{:S(2)}, u32[]{:S(2)}) async-start(bf16[32,8,768]{2,1,0:T(8,128)(2,1)} %bitcast.7), calls=%async_computation.1 | async-start | bytes 786432 | tf_op jit(solution)/shard_map/all_to_all | solution.py:158
  44.2 1.3 fusion.30
  45.5 2.5 %scatter_custom_fusion.1 = bf16[256,2048]{1,0:T(8,128)(2,1)} fusion(s32[128]{0:T(128)S(1)} %fusion.31, f32[16,2048]{1,0:T(8,128)S(1)} %convert_element_type.193, f32[128]{0:T(128)S(1)} %mul.98, bf16[]{:T(256)} %constant.147.clone.1), kind=kCustom, calls=%fused_computation.171 | custom fusion | flops 524288 | bytes 1180162 | tf_op jit(solution)/shard_map/scatter | solution.py:163
  48.1 1.3 all-to-all-done.1
  49.3 6.2 %all-to-all-start.2 = ((bf16[32,8,2048]{2,1,0:T(8,128)(2,1)}), bf16[32,8,2048]{2,1,0:T(8,128)(2,1)S(1)}, u32[]{:S(2)}, u32[]{:S(2)}) async-start(bf16[32,8,2048]{2,1,0:T(8,128)(2,1)} %bitcast.18), calls=%async_computation.2 | async-start | bytes 2097152 | tf_op jit(solution)/shard_map/all_to_all | solution.py:168
  56.4 30.3 %conditional.2 = (bf16[32,32,128]{2,1,0:T(8,128)(2,1)}) conditional(s32[]{:T(128)} %clamp.4, (s32[32]{0:T(128)S(1)}, bf16[32,32,128]{2,1,0:T(8,128)(2,1)S(1)}, s32[32]{0:T(128)S(1)}) %tuple.127, (s32[32]{0:T(128)S(1)}, bf16[32,32,128]{2,1,0:T(8,128)(2,1)S(1)}, s32[32]{0:T(128)S(1)}) %tuple.127, (s32[32]{0:T(128)S(1)}, ...), branch_computations={%region_7.8_spmd, %region_8.9_spmd, %region_9.10_spmd, %region_10.... | conditional | flops 2048 | bytes 2105904 | solution.py:137
  57.0 13.8 %collective-permute-start.9 = (bf16[18,32,128]{2,1,0:T(8,128)(2,1)S(1)}, bf16[18,32,128]{2,1,0:T(8,128)(2,1)S(1)}, u32[]{:S(2)}, u32[]{:S(2)}) collective-permute-start(bf16[18,32,128]{2,1,0:T(8,128)(2,1)S(1)} %gather_fusion.18), channel_id=1, source_target_pairs={{0,32},{32,0},{1,33},{33,1},{2,34},{34,2},{3,35},{35,3},{4,36},{36... | collective-permute-start | bytes 442376 | tf_op jit(solution)/shard_map/cond/branch_9_fun/ppermute | solution.py:131
  70.8 14.6 %collective-permute-done.9 = bf16[18,32,128]{2,1,0:T(8,128)(2,1)S(1)} collective-permute-done((bf16[18,32,128]{2,1,0:T(8,128)(2,1)S(1)}, bf16[18,32,128]{2,1,0:T(8,128)(2,1)S(1)}, u32[]{:S(2)}, u32[]{:S(2)}) %collective-permute-start.9) | collective-permute-done | bytes 147488 | tf_op jit(solution)/shard_map/cond/branch_9_fun/ppermute | solution.py:131
  85.4 1.3 gather_fusion.19
  87.8 4.5 %convolution_convert_fusion = bf16[1536,2048]{1,0:T(8,128)(2,1)} fusion(bf16[32,8,2048]{2,1,0:T(8,128)(2,1)S(1)} %all-to-all-done.2, bf16[256,768]{1,0:T(8,128)(2,1)S(1)} %get-tuple-element.399, bf16[256,768]{1,0:T(8,128)(2,1)S(1)} %get-tuple-element.398), kind=kOutput, calls=%fused_computation.148 | convolution fusion | flops 1615331328 | bytes 8126464 | tf_op jit(solution)/shard_map/dot_general | solution.py:182
  92.3 7.4 %all-to-all-start.3 = ((bf16[32,32,128]{2,1,0:T(8,128)(2,1)}), bf16[32,32,128]{2,1,0:T(8,128)(2,1)S(1)}, u32[]{:S(2)}, u32[]{:S(2)}) async-start(bf16[32,32,128]{2,1,0:T(8,128)(2,1)} %get-tuple-element.406), calls=%async_computation.3 | async-start | bytes 524288 | tf_op jit(solution)/shard_map/all_to_all | solution.py:189
  99.8 7.0 %all-to-all-done.3 = bf16[32,32,128]{2,1,0:T(8,128)(2,1)S(1)} async-done(((bf16[32,32,128]{2,1,0:T(8,128)(2,1)}), bf16[32,32,128]{2,1,0:T(8,128)(2,1)S(1)}, u32[]{:S(2)}, u32[]{:S(2)}) %all-to-all-start.3) | async-done | bytes 262176 | tf_op jit(solution)/shard_map/all_to_all | solution.py:189
  106.7 6.9 %all-gather.3.cloned.1.call-done = bf16[1,1536,2048]{2,1,0:T(8,128)(2,1)} async-done(((bf16[1,96,2048]{2,1,0:T(8,128)(2,1)}), bf16[1,1536,2048]{2,1,0:T(8,128)(2,1)}) %all-gather.3.cloned.1.call-update) | async-done | bytes 6291472 | tf_op jit(solution)/shard_map/all_gather | solution.py:147
  113.7 33.6 %conditional.3 = (bf16[32,64,128]{2,1,0:T(8,128)(2,1)}) conditional(s32[]{:T(128)} %clamp.4, (s32[32]{0:T(128)S(1)}, bf16[32,64,128]{2,1,0:T(8,128)(2,1)S(1)}, s32[32]{0:T(128)S(1)}) %tuple.131, (s32[32]{0:T(128)S(1)}, bf16[32,64,128]{2,1,0:T(8,128)(2,1)S(1)}, s32[32]{0:T(128)S(1)}) %tuple.131, (s32[32]{0:T(128)S(1)}, ...), branch_computations={%region_26.27_spmd, %region_27.28_spmd, %region_28.29_spmd, %regio... | conditional | flops 2048 | bytes 4203056 | solution.py:137
  114.3 8.6 %collective-permute-start.27 = (bf16[18,64,128]{2,1,0:T(8,128)(2,1)S(1)}, bf16[18,64,128]{2,1,0:T(8,128)(2,1)S(1)}, u32[]{:S(2)}, u32[]{:S(2)}) collective-permute-start(bf16[18,64,128]{2,1,0:T(8,128)(2,1)S(1)} %gather_fusion.54), channel_id=1, source_target_pairs={{0,32},{32,0},{1,33},{33,1},{2,34},{34,2},{3,35},{35,3},{4,36},{36... | collective-permute-start | bytes 884744 | tf_op jit(solution)/shard_map/cond/branch_9_fun/ppermute | solution.py:131
  122.9 22.9 %collective-permute-done.27 = bf16[18,64,128]{2,1,0:T(8,128)(2,1)S(1)} collective-permute-done((bf16[18,64,128]{2,1,0:T(8,128)(2,1)S(1)}, bf16[18,64,128]{2,1,0:T(8,128)(2,1)S(1)}, u32[]{:S(2)}, u32[]{:S(2)}) %collective-permute-start.27) | collective-permute-done | bytes 294944 | tf_op jit(solution)/shard_map/cond/branch_9_fun/ppermute | solution.py:131
  145.8 1.4 gather_fusion.55
  147.3 4.7 %convolution_convert_fusion.1 = bf16[256,1536]{1,0:T(8,128)(2,1)S(1)} fusion(bf16[1536,2048]{1,0:T(8,128)(2,1)} %bitcast.118, bf16[32,8,2048]{2,1,0:T(8,128)(2,1)S(1)} %all-to-all-done.2), kind=kOutput, calls=%fused_computation.149 | convolution fusion | flops 1611005952 | bytes 8126464 | tf_op jit(solution)/shard_map/dot_general | solution.py:198
  152.1 19.9 %all_to_all.35 = bf16[32,8,768]{2,1,0:T(8,128)(2,1)S(1)} all-to-all(bf16[32,8,768]{2,1,0:T(8,128)(2,1)S(1)} %fusion.20), channel_id=1, replica_groups=mesh['dp'=8,'zh'=2,'p'=32] {'p'}, dimensions={0} | all-to-all | bytes 786432 | tf_op jit(solution)/shard_map/all_to_all | solution.py:202
  172.0 6.1 %all-to-all-start.6 = ((bf16[32,64,128]{2,1,0:T(8,128)(2,1)}), bf16[32,64,128]{2,1,0:T(8,128)(2,1)S(1)}, u32[]{:S(2)}, u32[]{:S(2)}) async-start(bf16[32,64,128]{2,1,0:T(8,128)(2,1)} %get-tuple-element.407), calls=%async_computation.6 | async-start | bytes 1048576 | tf_op jit(solution)/shard_map/all_to_all | solution.py:206
  178.1 5.6 %fusion = bf16[32,8,2048]{2,1,0:T(8,128)(2,1)} fusion(bf16[1536,2048]{1,0:T(8,128)(2,1)} %bitcast.119, bf16[256,768]{1,0:T(8,128)(2,1)S(1)} %copy-done.4, bf16[256,768]{1,0:T(8,128)(2,1)S(1)} %copy-done.3), kind=kOutput, calls=%fused_computation.151 | convolution fusion | flops 1612709888 | bytes 8126464 | tf_op jit(solution)/shard_map/dot_general | solution.py:194
  183.7 3.8 %all-to-all-done.6 = bf16[32,64,128]{2,1,0:T(8,128)(2,1)S(1)} async-done(((bf16[32,64,128]{2,1,0:T(8,128)(2,1)}), bf16[32,64,128]{2,1,0:T(8,128)(2,1)S(1)}, u32[]{:S(2)}, u32[]{:S(2)}) %all-to-all-start.6) | async-done | bytes 524320 | tf_op jit(solution)/shard_map/all_to_all | solution.py:206
  187.5 6.2 %all-to-all-start.4 = ((bf16[32,8,2048]{2,1,0:T(8,128)(2,1)}), bf16[32,8,2048]{2,1,0:T(8,128)(2,1)S(1)}, u32[]{:S(2)}, u32[]{:S(2)}) async-start(bf16[32,8,2048]{2,1,0:T(8,128)(2,1)} %fusion), calls=%async_computation.4 | async-start | bytes 2097152 | tf_op jit(solution)/shard_map/all_to_all | solution.py:195
  195.7 1.5 gather_fusion.73
  197.2 4.7 %shard_map.129 = (bf16[1,96,2048]{2,1,0:T(8,128)(2,1)}, f32[1,96,2048]{2,1,0:T(8,128)}, f32[1,96,2048]{2,1,0:T(8,128)}) custom-call(s32[2]{0:T(128)} %pad_add_fusion.where_ref, bf16[1536,2048]{1,0:T(8,128)(2,1)} %bitcast.120, f32[1,96,2048]{2,1,0:T(8,128)} %first_ref.3, f32[1,96,2048]{2,1,0:T(8,128)} %second_ref.3, bf16[2,16,32,128]{3,2,1,0:T(8,128)(2,1)} %bitcast.125, ...), custom_call_target="tpu_custom_call" | custom-call | tf_op jit(solution)/shard_map/pallas_call | solution.py:87
  201.9 6.6 %all-to-all-done.4 = bf16[32,8,2048]{2,1,0:T(8,128)(2,1)S(1)} async-done(((bf16[32,8,2048]{2,1,0:T(8,128)(2,1)}), bf16[32,8,2048]{2,1,0:T(8,128)(2,1)S(1)}, u32[]{:S(2)}, u32[]{:S(2)}) %all-to-all-start.4) | async-done | bytes 1048608 | tf_op jit(solution)/shard_map/all_to_all | solution.py:195
  210.5 6.2 %reduce-scatter.2.cloned.1.call-done = bf16[96,2048]{1,0:T(8,128)(2,1)} async-done(((bf16[1536,2048]{1,0:T(8,128)(2,1)}), bf16[96,2048]{1,0:T(8,128)(2,1)}) %reduce-scatter.2.cloned.1.call-update) | async-done | bytes 393232 | tf_op jit(solution)/shard_map/reduce_scatter | solution.py:185
  216.7 3.2 %subtract_convert_fusion = (bf16[1,96,2048]{2,1,0:T(8,128)(2,1)}, f32[1,96,2048]{2,1,0:T(8,128)}, f32[1,96,2048]{2,1,0:T(8,128)}) fusion(bf16[1,96,2048]{2,1,0:T(8,128)(2,1)} %get-tuple-element.390, f32[1,96,2048]{2,1,0:T(8,128)} %get-tuple-element.391, bf16[96,2048]{1,0:T(8,128)(2,1)} %reduce-scatter.2.cloned.1.call-done, f32[1,96,2048]{2,1,0:T(8,128)} %get-tuple-element.392), kind=kLoop, calls=%fused_computation.170 | loop fusion | flops 2555904 | bytes 4325376 | tf_op jit(solution)/shard_map/convert_element_type | solution.py:25
  (53 shorter events, 11.7 us)
Async XLA Ops:
  7.2 25.8 %copy-start = (bf16[16,8,768]{2,1,0:T(8,128)(2,1)S(1)}, bf16[16,8,768]{2,1,0:T(8,128)(2,1)}, u32[]{:S(2)}) copy-start(bf16[16,8,768]{2,1,0:T(8,128)(2,1)} %param.47) | copy-start | bytes 589828
  7.2 49.1 %copy-start.6 = (s32[64]{0:T(128)S(1)}, s32[64]{0:T(128)}, u32[]{:S(2)}) copy-start(s32[64]{0:T(128)} %param.50) | copy-start | bytes 772
  7.2 38.3 %copy-start.5 = (bf16[16,2048]{1,0:T(8,128)(2,1)S(1)}, bf16[16,2048]{1,0:T(8,128)(2,1)}, u32[]{:S(2)}) copy-start(bf16[16,2048]{1,0:T(8,128)(2,1)} %param.48) | copy-start | bytes 196612
  7.2 106.5 %all-gather.3.cloned.1.call-start = ((), (), s32[]{:S(2)}) async-start(), calls=%async_computation.9 | async-start | bytes 6684672 | tf_op jit(solution)/shard_map/all_gather | solution.py:147
  11.4 21.5 %all-to-all-start = ((bf16[32,1,96,128]{3,2,1,0:T(8,128)(2,1)}), bf16[32,1,96,128]{3,2,1,0:T(8,128)(2,1)S(1)}, u32[]{:S(2)}, u32[]{:S(2)}) async-start(bf16[32,1,96,128]{3,2,1,0:T(8,128)(2,1)} %bitcast.123), calls=%async_computation | async-start | bytes 1572864 | tf_op jit(solution)/shard_map/all_to_all | solution.py:140
  34.8 14.5 %all-to-all-start.1 = ((bf16[32,8,768]{2,1,0:T(8,128)(2,1)}), bf16[32,8,768]{2,1,0:T(8,128)(2,1)S(1)}, u32[]{:S(2)}, u32[]{:S(2)}) async-start(bf16[32,8,768]{2,1,0:T(8,128)(2,1)} %bitcast.7), calls=%async_computation.1 | async-start | bytes 786432 | tf_op jit(solution)/shard_map/all_to_all | solution.py:158
  49.3 38.5 %all-to-all-start.2 = ((bf16[32,8,2048]{2,1,0:T(8,128)(2,1)}), bf16[32,8,2048]{2,1,0:T(8,128)(2,1)S(1)}, u32[]{:S(2)}, u32[]{:S(2)}) async-start(bf16[32,8,2048]{2,1,0:T(8,128)(2,1)} %bitcast.18), calls=%async_computation.2 | async-start | bytes 2097152 | tf_op jit(solution)/shard_map/all_to_all | solution.py:168
  55.5 161.2 %reduce-scatter.2.cloned.1.call-start = ((), (), s32[]{:S(2)}) async-start(), calls=%async_computation.8 | async-start | bytes 6684672 | tf_op jit(solution)/shard_map/reduce_scatter | solution.py:185
  57.0 28.4 %collective-permute-start.9 = (bf16[18,32,128]{2,1,0:T(8,128)(2,1)S(1)}, bf16[18,32,128]{2,1,0:T(8,128)(2,1)S(1)}, u32[]{:S(2)}, u32[]{:S(2)}) collective-permute-start(bf16[18,32,128]{2,1,0:T(8,128)(2,1)S(1)} %gather_fusion.18), channel_id=1, source_target_pairs={{0,32},{32,0},{1,33},{33,1},{2,34},{34,2},{3,35},{35,3},{4,36},{36... | collective-permute-start | bytes 442376 | tf_op jit(solution)/shard_map/cond/branch_9_fun/ppermute | solution.py:131
  92.3 14.4 %all-to-all-start.3 = ((bf16[32,32,128]{2,1,0:T(8,128)(2,1)}), bf16[32,32,128]{2,1,0:T(8,128)(2,1)S(1)}, u32[]{:S(2)}, u32[]{:S(2)}) async-start(bf16[32,32,128]{2,1,0:T(8,128)(2,1)} %get-tuple-element.406), calls=%async_computation.3 | async-start | bytes 524288 | tf_op jit(solution)/shard_map/all_to_all | solution.py:189
  106.7 6.9 %copy-start.2 = (bf16[32,32,128]{2,1,0:T(8,128)(2,1)}, bf16[32,32,128]{2,1,0:T(8,128)(2,1)S(1)}, u32[]{:S(2)}) copy-start(bf16[32,32,128]{2,1,0:T(8,128)(2,1)S(1)} %all-to-all-done.3) | copy-start | bytes 786436
  114.3 31.6 %collective-permute-start.27 = (bf16[18,64,128]{2,1,0:T(8,128)(2,1)S(1)}, bf16[18,64,128]{2,1,0:T(8,128)(2,1)S(1)}, u32[]{:S(2)}, u32[]{:S(2)}) collective-permute-start(bf16[18,64,128]{2,1,0:T(8,128)(2,1)S(1)} %gather_fusion.54), channel_id=1, source_target_pairs={{0,32},{32,0},{1,33},{33,1},{2,34},{34,2},{3,35},{35,3},{4,36},{36... | collective-permute-start | bytes 884744 | tf_op jit(solution)/shard_map/cond/branch_9_fun/ppermute | solution.py:131
  147.3 30.8 %copy-start.3 = (bf16[256,768]{1,0:T(8,128)(2,1)S(1)}, bf16[256,768]{1,0:T(8,128)(2,1)}, u32[]{:S(2)}) copy-start(bf16[256,768]{1,0:T(8,128)(2,1)} %get-tuple-element.396) | copy-start | bytes 1179652
  147.3 30.8 %copy-start.4 = (bf16[256,768]{1,0:T(8,128)(2,1)S(1)}, bf16[256,768]{1,0:T(8,128)(2,1)}, u32[]{:S(2)}) copy-start(bf16[256,768]{1,0:T(8,128)(2,1)} %get-tuple-element.397) | copy-start | bytes 1179652
  172.0 15.5 %all-to-all-start.6 = ((bf16[32,64,128]{2,1,0:T(8,128)(2,1)}), bf16[32,64,128]{2,1,0:T(8,128)(2,1)S(1)}, u32[]{:S(2)}, u32[]{:S(2)}) async-start(bf16[32,64,128]{2,1,0:T(8,128)(2,1)} %get-tuple-element.407), calls=%async_computation.6 | async-start | bytes 1048576 | tf_op jit(solution)/shard_map/all_to_all | solution.py:206
  187.5 9.7 %copy-start.1 = (bf16[32,64,128]{2,1,0:T(8,128)(2,1)}, bf16[32,64,128]{2,1,0:T(8,128)(2,1)S(1)}, u32[]{:S(2)}) copy-start(bf16[32,64,128]{2,1,0:T(8,128)(2,1)S(1)} %all-to-all-done.6) | copy-start | bytes 1572868
  187.5 21.0 %all-to-all-start.4 = ((bf16[32,8,2048]{2,1,0:T(8,128)(2,1)}), bf16[32,8,2048]{2,1,0:T(8,128)(2,1)S(1)}, u32[]{:S(2)}, u32[]{:S(2)}) async-start(bf16[32,8,2048]{2,1,0:T(8,128)(2,1)} %fusion), calls=%async_computation.4 | async-start | bytes 2097152 | tf_op jit(solution)/shard_map/all_to_all | solution.py:195
Sparse Core Ops, SparseCore 0:
  10.1 103.4 all-gather.2
  116.5 100.1 reduce-scatter.1
